TPU v7x, 32 devices: a whole 2x2x4 slice. The times are simulated.
32 devices in a mesh: blk: 8 (over z, x), grp: 4 (over y, core).
Axes of the slice: x: 2, y: 2, z: 4, core: 2. Of those that a mesh axis runs over, the one named last changes fastest.
Arguments:
- flow: float32 [384, 5, 4096], P(('blk', 'grp')), may hold values from -3 to 6, as said below
- adjoint: float32 [384, 5, 4096], P(('blk', 'grp')), may hold values from -6 to 6
- cut_flag: int32 [384, 4096], P(('blk', 'grp')), may hold values 0 or 1
- lateral_owner: int32 [384, 4, 1], P(('blk', 'grp')), may hold values from 0 to 7; in each aligned block of 48 rows (0 to 47, 48 to 95, ..., all dimensions but the last counted through in order) at most 9 rows name the same one
- lateral_link: int32 [384, 4], P(('blk', 'grp')), may hold values from 0 to 59
- vertical_link: int32 [384, 2], P(('blk', 'grp')), may hold values from 0 to 59
Outputs:
- indicator: float32 [384, 4096], P(('blk', 'grp'))
Inputs may be any that keep to these rules, and one draw needn't show every extreme that they name: `flow`: density lies between 1 and 2, pressure between 1 and 2, every velocity component between -1.25 and 1.25. `lateral_owner`: among the faces 0 to 3 of the blocks of one device, at most 9 have their neighbour on any one blk index, and in every draw some device reaches 9.
All inputs are finite; a program needn't handle non-finite values. No bound on the sum of `cut_flag` on one device may be relied on, other than what follows from the above.
Results may differ from a plain program's by a relative error of at most 0.0003.
Values sent between devices are 32-bit elements; how exact they have to be, the bound alone decides.
A program may use at most 128 MiB of HBM per device.

v0:
```python
import jax
import jax.numpy as jnp
from jax import lax
from jax.sharding import PartitionSpec as P

EDGE = 16


HEAT_RATIO = 1.4
ENTROPY_FIX = 0.2
FREESTREAM = (1.0, 0.0, 0.0, 0.3, 1.0)


def extended(cells, sides, width):
    for axis, dim in sides:
        count = lax.axis_size(axis)
        ends = count - 1
        head = lax.slice_in_dim(cells, 0, width, axis=dim)
        tail = lax.slice_in_dim(cells, cells.shape[dim] - width, cells.shape[dim], axis=dim)
        cells = jnp.concatenate(
            [
                lax.ppermute(tail, axis, [(i, (i + 1) % count) for i in range(ends)]),
                cells,
                lax.ppermute(head, axis, [((i + 1) % count, i) for i in range(ends)]),
            ],
            axis=dim,
        )
    return cells


def primitive(conserved):
    density = conserved[:, 0]
    velocity = conserved[:, 1:4] / density[:, None]
    pressure = (HEAT_RATIO - 1.0) * (
        conserved[:, 4] - 0.5 * density * jnp.sum(velocity * velocity, axis=1)
    )
    return jnp.concatenate([density[:, None], velocity, pressure[:, None]], axis=1)


def minmod(first_diff, second_diff):
    return jnp.where(
        first_diff * second_diff > 0.0,
        jnp.sign(first_diff) * jnp.minimum(jnp.abs(first_diff), jnp.abs(second_diff)),
        0.0,
    )


def harten(wave_rate, spread):
    return jnp.where(
        wave_rate < spread, (wave_rate * wave_rate + spread * spread) / (2.0 * spread), wave_rate
    )


def roe_flux(left_state, right_state, normal_axis):
    left_rho = left_state[0]
    right_rho = right_state[0]
    left_vel = left_state[1:4]
    right_vel = right_state[1:4]
    left_press = left_state[4]
    right_press = right_state[4]
    factor = HEAT_RATIO / (HEAT_RATIO - 1.0)
    left_enth = factor * left_press / left_rho + 0.5 * jnp.sum(left_vel * left_vel, axis=0)
    right_enth = factor * right_press / right_rho + 0.5 * jnp.sum(right_vel * right_vel, axis=0)
    left_root = jnp.sqrt(left_rho)
    right_root = jnp.sqrt(right_rho)
    weight_sum = left_root + right_root
    mean_vel = (left_root * left_vel + right_root * right_vel) / weight_sum
    mean_enth = (left_root * left_enth + right_root * right_enth) / weight_sum
    speed_sq = jnp.sum(mean_vel * mean_vel, axis=0)
    sound_sq = (HEAT_RATIO - 1.0) * (mean_enth - 0.5 * speed_sq)
    sound_speed = jnp.sqrt(sound_sq)
    mean_rho = left_root * right_root
    normal = mean_vel[normal_axis]
    jump_vel = right_vel - left_vel
    jump_rho = right_rho - left_rho
    jump_press = right_press - left_press
    jump_normal = jump_vel[normal_axis]
    wave_slow = (jump_press - mean_rho * sound_speed * jump_normal) / (2.0 * sound_sq)
    wave_fast = (jump_press + mean_rho * sound_speed * jump_normal) / (2.0 * sound_sq)
    wave_entropy = jump_rho - jump_press / sound_sq
    spread = ENTROPY_FIX * sound_speed
    slow_part = harten(jnp.abs(normal - sound_speed), spread) * wave_slow
    fast_part = harten(jnp.abs(normal + sound_speed), spread) * wave_fast
    mid_part = jnp.abs(normal) * wave_entropy
    shear_part = jnp.abs(normal) * mean_rho
    unit_vector = [1.0 if axis_no == normal_axis else 0.0 for axis_no in range(3)]
    shear_jump = [jump_vel[axis_no] - jump_normal * unit_vector[axis_no] for axis_no in range(3)]
    diss_mass = slow_part + fast_part + mid_part
    diss_mom = [
        slow_part * (mean_vel[axis_no] - sound_speed * unit_vector[axis_no])
        + fast_part * (mean_vel[axis_no] + sound_speed * unit_vector[axis_no])
        + mid_part * mean_vel[axis_no]
        + shear_part * shear_jump[axis_no]
        for axis_no in range(3)
    ]
    diss_energy = (
        slow_part * (mean_enth - normal * sound_speed)
        + fast_part * (mean_enth + normal * sound_speed)
        + mid_part * 0.5 * speed_sq
        + shear_part
        * (mean_vel[0] * shear_jump[0] + mean_vel[1] * shear_jump[1] + mean_vel[2] * shear_jump[2])
    )
    left_normal = left_vel[normal_axis]
    right_normal = right_vel[normal_axis]
    mass_flux = 0.5 * (left_rho * left_normal + right_rho * right_normal) - 0.5 * diss_mass
    momentum = [
        0.5
        * (
            left_rho * left_normal * left_vel[axis_no]
            + right_rho * right_normal * right_vel[axis_no]
            + (left_press + right_press) * unit_vector[axis_no]
        )
        - 0.5 * diss_mom[axis_no]
        for axis_no in range(3)
    ]
    energy = (
        0.5 * (left_rho * left_normal * left_enth + right_rho * right_normal * right_enth)
        - 0.5 * diss_energy
    )
    return jnp.stack([mass_flux] + momentum + [energy], axis=0)


def wall_flux(pressure, normal_axis):
    nothing = jnp.zeros_like(pressure)
    parts = [pressure if axis_no == normal_axis else nothing for axis_no in range(3)]
    return jnp.stack([nothing] + parts + [nothing], axis=0)


def face_flux(left_state, right_state, left_solid, right_solid, normal_axis):
    roe_value = roe_flux(left_state, right_state, normal_axis)
    from_left = (right_solid > 0.5) & (left_solid < 0.5)
    from_right = (left_solid > 0.5) & (right_solid < 0.5)
    return jnp.where(
        from_left,
        wall_flux(left_state[4], normal_axis),
        jnp.where(from_right, wall_flux(right_state[4], normal_axis), roe_value),
    )


def faces_of(values, edge_cells):
    plane_size = edge_cells * edge_cells
    face_shape = values.shape[:2] + (plane_size,)
    return jnp.stack(
        [
            values[:, :, 0],
            values[:, :, edge_cells - 1],
            values[:, :, :, :edge_cells].reshape(face_shape),
            values[:, :, :, plane_size - edge_cells :].reshape(face_shape),
            values[:, :, :, 0::edge_cells].reshape(face_shape),
            values[:, :, :, edge_cells - 1 :: edge_cells].reshape(face_shape),
        ],
        axis=1,
    )


def select_face(face_slab, level_code):
    channels = face_slab.shape[0]
    half_edge = EDGE // 2
    square = face_slab.reshape(channels, EDGE, EDGE)
    quarter_code = jnp.minimum(level_code, 3)
    anchor = jnp.zeros((), jnp.int32)
    first_start = quarter_code // 2 * half_edge
    second_start = quarter_code % 2 * half_edge
    quarter = lax.dynamic_slice(
        square, (anchor, first_start, second_start), (channels, half_edge, half_edge)
    )
    widened = jnp.broadcast_to(quarter[:, :, None, :, None], (channels, half_edge, 2, half_edge, 2))
    return jnp.where(level_code == 4, face_slab, widened.reshape(channels, EDGE * EDGE))


def shifted(values, ghosts, edge_cells):
    channels = values.shape[0]
    plane_size = edge_cells * edge_cells
    depth_index = lax.broadcasted_iota(jnp.int32, (1, 1, plane_size), 2) % edge_cells
    lower_x = jnp.concatenate([ghosts[0][:, None], values[:, :-1]], axis=1)
    upper_x = jnp.concatenate([values[:, 1:], ghosts[1][:, None]], axis=1)
    lower_y = jnp.concatenate(
        [
            ghosts[2].reshape(channels, edge_cells, edge_cells),
            values[:, :, : plane_size - edge_cells],
        ],
        axis=2,
    )
    upper_y = jnp.concatenate(
        [values[:, :, edge_cells:], ghosts[3].reshape(channels, edge_cells, edge_cells)], axis=2
    )
    low_rim = jnp.repeat(ghosts[4].reshape(channels, edge_cells, edge_cells), edge_cells, axis=2)
    high_rim = jnp.repeat(ghosts[5].reshape(channels, edge_cells, edge_cells), edge_cells, axis=2)
    lower_z = jnp.where(
        depth_index == 0, low_rim, jnp.concatenate([values[:, :, :1], values[:, :, :-1]], axis=2)
    )
    upper_z = jnp.where(
        depth_index == edge_cells - 1,
        high_rim,
        jnp.concatenate([values[:, :, 1:], values[:, :, -1:]], axis=2),
    )
    return ((lower_x, upper_x), (lower_y, upper_y), (lower_z, upper_z))


def plane_tables(edge_cells):
    plane_size = edge_cells * edge_cells
    fine_edge = 2 * edge_cells
    coarse_index = lax.broadcasted_iota(jnp.int32, (plane_size, 4 * plane_size), 0)
    fine_index = lax.broadcasted_iota(jnp.int32, (plane_size, 4 * plane_size), 1)
    fine_row = fine_index // fine_edge
    fine_col = fine_index % fine_edge
    parent = fine_row // 2 * edge_cells + fine_col // 2 == coarse_index
    ones_table = jnp.where(parent, 1.0, 0.0).astype(jnp.float32)
    row_table = jnp.where(parent, jnp.where(fine_row % 2 == 0, -0.25, 0.25), 0.0).astype(
        jnp.float32
    )
    col_table = jnp.where(parent, jnp.where(fine_col % 2 == 0, -0.25, 0.25), 0.0).astype(
        jnp.float32
    )
    return (ones_table, jnp.concatenate([ones_table, row_table, col_table], axis=0))


def prolong(values, ghosts, edge_cells, expand_table):
    channels = values.shape[0]
    plane_size = edge_cells * edge_cells
    slopes = [
        minmod(upper_side - values, values - lower_side)
        for lower_side, upper_side in shifted(values, ghosts, edge_cells)
    ]
    layer_sign = jnp.where(
        lax.broadcasted_iota(jnp.int32, (1, 2 * edge_cells, 1), 1) % 2 == 0, -0.25, 0.25
    )
    first_term = jnp.repeat(values, 2, axis=1) + jnp.repeat(slopes[0], 2, axis=1) * layer_sign
    stacked = jnp.concatenate(
        [first_term, jnp.repeat(slopes[1], 2, axis=1), jnp.repeat(slopes[2], 2, axis=1)], axis=2
    )
    fine_field = jnp.dot(
        stacked.reshape(channels * 2 * edge_cells, 3 * plane_size),
        expand_table,
        precision=lax.Precision.HIGHEST,
        preferred_element_type=jnp.float32,
    )
    return fine_field.reshape(channels, 2 * edge_cells, 4 * plane_size)


def residual(fine_field, fine_ghosts, solid_mask, size_fine):
    channels = fine_field.shape[0]
    plane_size = size_fine * size_fine
    depth_index = lax.broadcasted_iota(jnp.int32, (1, plane_size), 1) % size_fine
    rim_x = jnp.zeros((1, plane_size), jnp.float32)
    left_state = jnp.concatenate([fine_ghosts[0][:, None], fine_field], axis=1)
    right_state = jnp.concatenate([fine_field, fine_ghosts[1][:, None]], axis=1)
    flux_x = face_flux(
        left_state,
        right_state,
        jnp.concatenate([rim_x, solid_mask], axis=0),
        jnp.concatenate([solid_mask, rim_x], axis=0),
        0,
    )
    summed = flux_x[:, 1:] - flux_x[:, :-1]
    rim_y = jnp.zeros((size_fine, size_fine), jnp.float32)
    left_state = jnp.concatenate(
        [fine_ghosts[2].reshape(channels, size_fine, size_fine), fine_field], axis=2
    )
    right_state = jnp.concatenate(
        [fine_field, fine_ghosts[3].reshape(channels, size_fine, size_fine)], axis=2
    )
    flux_y = face_flux(
        left_state,
        right_state,
        jnp.concatenate([rim_y, solid_mask], axis=1),
        jnp.concatenate([solid_mask, rim_y], axis=1),
        1,
    )
    summed = summed + flux_y[:, :, size_fine:] - flux_y[:, :, :plane_size]
    low_rim = jnp.repeat(fine_ghosts[4].reshape(channels, size_fine, size_fine), size_fine, axis=2)
    lower_state = jnp.where(
        depth_index == 0,
        low_rim,
        jnp.concatenate([fine_field[:, :, :1], fine_field[:, :, :-1]], axis=2),
    )
    lower_solid = jnp.where(
        depth_index == 0, 0.0, jnp.concatenate([solid_mask[:, :1], solid_mask[:, :-1]], axis=1)
    )
    flux_low = face_flux(lower_state, fine_field, lower_solid, solid_mask, 2)
    top_state = fine_field[:, :, size_fine - 1 :: size_fine]
    flux_top = face_flux(
        top_state,
        fine_ghosts[5].reshape(channels, size_fine, size_fine),
        solid_mask[:, size_fine - 1 :: size_fine],
        rim_y,
        2,
    )
    flux_high = jnp.where(
        depth_index == size_fine - 1,
        jnp.repeat(flux_top, size_fine, axis=2),
        jnp.concatenate([flux_low[:, :, 1:], flux_low[:, :, -1:]], axis=2),
    )
    summed = summed + flux_high - flux_low
    return jnp.where(solid_mask > 0.5, 0.0, summed)


def make_indicator(ones_table, expand_table):

    def block_indicator(operands):
        flow_prim, adjoint_block, ghosts, flags = operands
        plane_size = EDGE * EDGE
        fine_flow = prolong(
            flow_prim.reshape(5, EDGE, plane_size), ghosts[:, :5], EDGE, expand_table
        )
        fine_adjoint = prolong(
            adjoint_block.reshape(5, EDGE, plane_size), ghosts[:, 5:], EDGE, expand_table
        )
        wide_ghosts = jnp.dot(
            ghosts[:, :5].reshape(30, plane_size),
            ones_table,
            precision=lax.Precision.HIGHEST,
            preferred_element_type=jnp.float32,
        ).reshape(6, 5, 4 * plane_size)
        flag_rows = jnp.repeat(flags.astype(jnp.float32).reshape(EDGE, plane_size), 2, axis=0)
        solid_mask = jnp.dot(
            flag_rows,
            ones_table,
            precision=lax.Precision.HIGHEST,
            preferred_element_type=jnp.float32,
        )
        fine_residual = residual(fine_flow, wide_ghosts, solid_mask, 2 * EDGE)
        weighted = jnp.sum(fine_adjoint * fine_residual, axis=0)
        paired = weighted[0::2] + weighted[1::2]
        coarse = jnp.dot(
            paired,
            ones_table.T,
            precision=lax.Precision.HIGHEST,
            preferred_element_type=jnp.float32,
        )
        return jnp.abs(coarse).reshape(EDGE * EDGE * EDGE)

    return block_indicator


def local(flow, adjoint, cut_flag, lateral_owner, lateral_link, vertical_link):
    blocks = flow.shape[0]
    plane_size = EDGE * EDGE
    peer_count = lax.axis_size("blk")
    capacity = max(2, 6 * blocks // peer_count)
    primitives = primitive(flow)
    coarse_both = jnp.concatenate([primitives, adjoint], axis=1).reshape(
        blocks, 10, EDGE, plane_size
    )
    face_all = faces_of(coarse_both, EDGE)
    owners = lateral_owner[:, :, 0].reshape(-1)
    lateral_codes = lateral_link.reshape(-1)
    far_sides = jnp.tile(jnp.array([1, 0, 3, 2], jnp.int32), blocks)
    requested = (lateral_codes // 5 * 4 + far_sides) * 5 + lateral_codes % 5
    matches = (owners[:, None] == jnp.arange(peer_count, dtype=jnp.int32)[None, :]).astype(
        jnp.int32
    )
    before = jnp.cumsum(matches, axis=0) - matches
    slot_pos = jnp.sum(before * matches, axis=1)
    requests = jnp.full((peer_count, capacity), -1, jnp.int32).at[owners, slot_pos].set(requested)
    wanted = lax.all_to_all(requests, "blk", split_axis=0, concat_axis=0, tiled=True)
    wanted_flat = wanted.reshape(-1)
    is_valid = wanted_flat >= 0
    safe_code = jnp.maximum(wanted_flat, 0)
    face_slabs = face_all[safe_code // 20, safe_code // 5 % 4]
    chosen = jax.vmap(select_face)(face_slabs, safe_code % 5)
    chosen = jnp.where(is_valid[:, None, None], chosen, 0.0)
    replies = chosen.reshape(wanted.shape + (10, plane_size))
    returned = lax.all_to_all(replies, "blk", split_axis=0, concat_axis=0, tiled=True)
    lateral = returned[owners, slot_pos].reshape(blocks, 4, 10, plane_size)
    stacked = jnp.stack([face_all[:, 4], face_all[:, 5]], axis=0)
    beside_all = extended(stacked, (("grp", 0),), 1)
    region = lax.axis_index("grp")
    last_region = lax.axis_size("grp") - 1
    lower_ghost = jax.vmap(select_face)(
        beside_all[0][vertical_link[:, 0] // 5], vertical_link[:, 0] % 5
    )
    upper_ghost = jax.vmap(select_face)(
        beside_all[3][vertical_link[:, 1] // 5], vertical_link[:, 1] % 5
    )
    state = jnp.array(FREESTREAM, jnp.float32)
    farfield_layer = jnp.concatenate(
        [
            jnp.broadcast_to(state[:, None], (5, plane_size)),
            jnp.zeros((5, plane_size), jnp.float32),
        ],
        axis=0,
    )
    lower_ghost = jnp.where(region == 0, farfield_layer, lower_ghost)
    upper_ghost = jnp.where(region == last_region, farfield_layer, upper_ghost)
    ghosts = jnp.concatenate([lateral, lower_ghost[:, None], upper_ghost[:, None]], axis=1)
    ones_table, expand_table = plane_tables(EDGE)
    return lax.map(
        make_indicator(ones_table, expand_table), (primitives, adjoint, ghosts, cut_flag)
    )


def solution(mesh):
    in_specs = (
        P(("blk", "grp"), None, None),
        P(("blk", "grp"), None, None),
        P(("blk", "grp"), None),
        P(("blk", "grp"), None, None),
        P(("blk", "grp"), None),
        P(("blk", "grp"), None),
    )
    out_specs = P(("blk", "grp"), None)
    return jax.shard_map(local, mesh=mesh, in_specs=in_specs, out_specs=out_specs, check_vma=False)
```

profile of v0, /device:TPU:14, one launch (start us, length us, event | category | flops | bytes accessed | tf_op | source)
XLA Modules:
  0.0 823.9 jit_solution(17349719856498172841)
XLA Ops:
  9.2 8.2 slice.1011
  17.3 2.9 copy.168
  20.3 2.3 reshape.1182
  24.5 8.0 slice.1010
  32.5 3.0 copy.167
  35.5 2.3 reshape.1184
  37.8 3.6 collective-permute-start.1
  43.4 7.8 scatter_fusion
  51.2 6.4 all-to-all-start
  58.3 2.2 fusion.306
  67.0 2.1 copy.165
  77.5 5.5 copy.170
  83.0 9.1 %gather_fusion.4 = f32[72,10,8,8]{1,0,3,2:T(8,128)S(1)} fusion(f32[72,10,16,16]{1,0,3,2:T(8,128)} %bitcast.577, s32[72]{0:T(128)S(1)} %get-tuple-element.471), kind=kCustom, calls=%fused_computation.4 | custom fusion | bytes 369792 | tf_op jit(solution)/shard_map/vmap()/gather | solution.py:164
  94.9 6.3 reshape.1088
  101.2 7.1 copy.143
  109.6 6.5 all-to-all-start.1
  116.2 3.3 pad_maximum_fusion.16
  124.0 2.1 gather_fusion.5
  129.2 2.2 gather_fusion.3
  131.4 2.2 copy.187
  133.6 2.1 gather_fusion.6
  142.0 681.7 %while.15 = (s32[]{:T(128)}, f32[12,4096]{1,0:T(8,128)}, f32[12,5,4096]{2,0,1:T(8,128)}, f32[12,6,10,256]{3,1,0,2:T(8,128)S(1)}, f32[768,1024]{1,0:T(8,128)}, /*...) while((s32[]{:T(128)}, f32[12,4096]{1,0:T(8,128)}, ...), condition=%wide.region_18.19_spmd.clone.clone, body=%wide.region_4.18_spmd.clone.clone.sunk | while | flops 3323658496 | bytes 116343456 | solution.py:388
  152.3 3.9 fusion.370
  183.1 2.2 multiply_select_fusion.9
  191.4 4.8 fusion.395
  209.1 3.9 fusion.370
  228.5 2.1 reshape.1255
  239.9 2.2 multiply_select_fusion.9
  248.2 4.8 fusion.395
  265.9 3.9 fusion.370
  285.3 2.1 reshape.1255
  296.7 2.2 multiply_select_fusion.9
  305.0 4.8 fusion.395
  322.7 3.9 fusion.370
  342.1 2.1 reshape.1255
  353.5 2.2 multiply_select_fusion.9
  361.8 4.8 fusion.395
  379.5 3.9 fusion.370
  398.9 2.1 reshape.1255
  410.3 2.2 multiply_select_fusion.9
  418.6 4.8 fusion.395
  436.3 3.9 fusion.370
  455.7 2.1 reshape.1255
  467.0 2.2 multiply_select_fusion.9
  475.4 4.8 fusion.395
  493.0 3.9 fusion.370
  512.5 2.1 reshape.1255
  523.8 2.2 multiply_select_fusion.9
  532.2 4.8 fusion.395
  549.8 3.9 fusion.370
  580.6 2.2 multiply_select_fusion.9
  589.0 4.8 fusion.395
  606.6 3.9 fusion.370
  637.4 2.2 multiply_select_fusion.9
  645.8 4.8 fusion.395
  663.4 3.9 fusion.370
  694.2 2.2 multiply_select_fusion.9
  702.6 4.8 fusion.395
  720.2 3.9 fusion.370
  751.0 2.2 multiply_select_fusion.9
  759.4 4.8 fusion.395
  777.0 3.9 fusion.370
  807.8 2.2 multiply_select_fusion.9
  816.1 4.8 fusion.395
  (2454 shorter events, 573.2 us)
Async XLA Ops:
  22.5 98.7 %collective-permute-start = (f32[1,12,10,256]{3,2,1,0:T(8,128)}, f32[1,12,10,256]{3,2,1,0:T(8,128)}, u32[]{:S(2)}, u32[]{:S(2)}) collective-permute-start(f32[1,12,10,256]{3,2,1,0:T(8,128)} %reshape.1182), channel_id=1, source_target_pairs={{0,1},{1,2},{2,3},{4,5},{5,6},{6,7},{8,9},{9,10},{10,11},{12,13},{... | collective-permute-start | bytes 368648 | tf_op jit(solution)/shard_map/ppermute | solution.py:22
  32.5 8.9 %copy-start.51 = (s32[12,4,1]{0,2,1:T(1,128)S(1)}, s32[12,4,1]{0,2,1:T(1,128)}, u32[]{:S(2)}) copy-start(s32[12,4,1]{0,2,1:T(1,128)} %param.13) | copy-start | bytes 580
  32.5 9.2 %copy-start.39 = (s32[12,4]{0,1:T(4,128)S(1)}, s32[12,4]{0,1:T(4,128)}, u32[]{:S(2)}) copy-start(s32[12,4]{0,1:T(4,128)} %param.14) | copy-start | bytes 580
  32.5 9.8 %copy-start.53 = (s32[4]{0:T(128)S(1)}, s32[4]{0:T(128)}, u32[]{:S(2)}) copy-start(s32[4]{0:T(128)} %constant.411.clone) | copy-start | bytes 52
  37.8 91.4 %collective-permute-start.1 = (f32[1,12,10,256]{3,2,1,0:T(8,128)}, f32[1,12,10,256]{3,2,1,0:T(8,128)}, u32[]{:S(2)}, u32[]{:S(2)}) collective-permute-start(f32[1,12,10,256]{3,2,1,0:T(8,128)} %reshape.1184), channel_id=1, source_target_pairs={{1,0},{2,1},{3,2},{5,4},{6,5},{7,6},{9,8},{10,9},{11,10},{13,12},{... | collective-permute-start | bytes 368648 | tf_op jit(solution)/shard_map/ppermute | solution.py:24
  51.2 23.7 %all-to-all-start = ((s32[8,1,9]{2,1,0:T(1,128)}), s32[8,1,9]{2,1,0:T(1,128)S(1)}, u32[]{:S(2)}, u32[]{:S(2)}) async-start(s32[8,1,9]{2,1,0:T(1,128)} %bitcast.3), calls=%async_computation | async-start | bytes 8192 | tf_op jit(solution)/shard_map/all_to_all | solution.py:356
  101.2 7.2 copy-start.40
  101.2 7.2 copy-start.41
  109.6 6.5 copy-start.6
  109.6 6.5 copy-start.7
  109.6 30.8 %all-to-all-start.1 = ((f32[8,9,10,256]{3,2,1,0:T(8,128)}), f32[8,9,10,256]{3,2,1,0:T(8,128)S(1)}, u32[]{:S(2)}, u32[]{:S(2)}) async-start(f32[8,9,10,256]{3,2,1,0:T(8,128)} %select_select_fusion.4), calls=%async_computation.1 | async-start | bytes 2359296 | tf_op jit(solution)/shard_map/all_to_all | solution.py:364
  162.2 12.4 %copy-start.1 = (f32[5,32,1024]{2,1,0:T(8,128)}, f32[5,32,1024]{2,1,0:T(8,128)S(1)}, u32[]{:S(2)}) copy-start(f32[5,32,1024]{2,1,0:T(8,128)S(1)} %fusion.377) | copy-start | bytes 1966084 | tf_op jit(solution)/shard_map/while
  177.4 5.7 copy-start.21
  183.1 8.3 %copy-start = (f32[768,1024]{1,0:T(8,128)S(1)}, f32[768,1024]{1,0:T(8,128)}, u32[]{:S(2)}) copy-start(f32[768,1024]{1,0:T(8,128)} %get-tuple-element.860) | copy-start | bytes 9437188 | tf_op jit(solution)/shard_map/while
  191.4 4.9 copy-start.29
  191.4 4.9 copy-start.31
  191.4 4.9 copy-start.34
  191.4 4.9 copy-start.37
  191.4 4.9 copy-start.44
  191.4 4.9 copy-start.47
  219.0 12.4 %copy-start.1 = (f32[5,32,1024]{2,1,0:T(8,128)}, f32[5,32,1024]{2,1,0:T(8,128)S(1)}, u32[]{:S(2)}) copy-start(f32[5,32,1024]{2,1,0:T(8,128)S(1)} %fusion.377) | copy-start | bytes 1966084 | tf_op jit(solution)/shard_map/while
  234.2 5.7 copy-start.21
  239.9 8.3 %copy-start = (f32[768,1024]{1,0:T(8,128)S(1)}, f32[768,1024]{1,0:T(8,128)}, u32[]{:S(2)}) copy-start(f32[768,1024]{1,0:T(8,128)} %get-tuple-element.860) | copy-start | bytes 9437188 | tf_op jit(solution)/shard_map/while
  248.2 4.9 copy-start.29
  248.2 4.9 copy-start.31
  248.2 4.9 copy-start.34
  248.2 4.9 copy-start.37
  248.2 4.9 copy-start.44
  248.2 4.9 copy-start.47
  275.8 12.4 %copy-start.1 = (f32[5,32,1024]{2,1,0:T(8,128)}, f32[5,32,1024]{2,1,0:T(8,128)S(1)}, u32[]{:S(2)}) copy-start(f32[5,32,1024]{2,1,0:T(8,128)S(1)} %fusion.377) | copy-start | bytes 1966084 | tf_op jit(solution)/shard_map/while
  291.0 5.7 copy-start.21
  296.7 8.3 %copy-start = (f32[768,1024]{1,0:T(8,128)S(1)}, f32[768,1024]{1,0:T(8,128)}, u32[]{:S(2)}) copy-start(f32[768,1024]{1,0:T(8,128)} %get-tuple-element.860) | copy-start | bytes 9437188 | tf_op jit(solution)/shard_map/while
  305.0 4.9 copy-start.29
  305.0 4.9 copy-start.31
  305.0 4.9 copy-start.34
  305.0 4.9 copy-start.37
  305.0 4.9 copy-start.44
  332.6 12.4 %copy-start.1 = (f32[5,32,1024]{2,1,0:T(8,128)}, f32[5,32,1024]{2,1,0:T(8,128)S(1)}, u32[]{:S(2)}) copy-start(f32[5,32,1024]{2,1,0:T(8,128)S(1)} %fusion.377) | copy-start | bytes 1966084 | tf_op jit(solution)/shard_map/while
  347.8 5.7 copy-start.21
  353.5 8.3 %copy-start = (f32[768,1024]{1,0:T(8,128)S(1)}, f32[768,1024]{1,0:T(8,128)}, u32[]{:S(2)}) copy-start(f32[768,1024]{1,0:T(8,128)} %get-tuple-element.860) | copy-start | bytes 9437188 | tf_op jit(solution)/shard_map/while
  389.4 12.4 %copy-start.1 = (f32[5,32,1024]{2,1,0:T(8,128)}, f32[5,32,1024]{2,1,0:T(8,128)S(1)}, u32[]{:S(2)}) copy-start(f32[5,32,1024]{2,1,0:T(8,128)S(1)} %fusion.377) | copy-start | bytes 1966084 | tf_op jit(solution)/shard_map/while
  404.6 5.7 copy-start.21
  410.3 8.3 %copy-start = (f32[768,1024]{1,0:T(8,128)S(1)}, f32[768,1024]{1,0:T(8,128)}, u32[]{:S(2)}) copy-start(f32[768,1024]{1,0:T(8,128)} %get-tuple-element.860) | copy-start | bytes 9437188 | tf_op jit(solution)/shard_map/while
  446.1 12.4 %copy-start.1 = (f32[5,32,1024]{2,1,0:T(8,128)}, f32[5,32,1024]{2,1,0:T(8,128)S(1)}, u32[]{:S(2)}) copy-start(f32[5,32,1024]{2,1,0:T(8,128)S(1)} %fusion.377) | copy-start | bytes 1966084 | tf_op jit(solution)/shard_map/while
  461.4 5.7 copy-start.21
  467.0 8.3 %copy-start = (f32[768,1024]{1,0:T(8,128)S(1)}, f32[768,1024]{1,0:T(8,128)}, u32[]{:S(2)}) copy-start(f32[768,1024]{1,0:T(8,128)} %get-tuple-element.860) | copy-start | bytes 9437188 | tf_op jit(solution)/shard_map/while
  502.9 12.4 %copy-start.1 = (f32[5,32,1024]{2,1,0:T(8,128)}, f32[5,32,1024]{2,1,0:T(8,128)S(1)}, u32[]{:S(2)}) copy-start(f32[5,32,1024]{2,1,0:T(8,128)S(1)} %fusion.377) | copy-start | bytes 1966084 | tf_op jit(solution)/shard_map/while
  518.2 5.7 copy-start.21
  523.8 8.3 %copy-start = (f32[768,1024]{1,0:T(8,128)S(1)}, f32[768,1024]{1,0:T(8,128)}, u32[]{:S(2)}) copy-start(f32[768,1024]{1,0:T(8,128)} %get-tuple-element.860) | copy-start | bytes 9437188 | tf_op jit(solution)/shard_map/while
  559.7 12.4 %copy-start.1 = (f32[5,32,1024]{2,1,0:T(8,128)}, f32[5,32,1024]{2,1,0:T(8,128)S(1)}, u32[]{:S(2)}) copy-start(f32[5,32,1024]{2,1,0:T(8,128)S(1)} %fusion.377) | copy-start | bytes 1966084 | tf_op jit(solution)/shard_map/while
  575.0 5.7 copy-start.21
  580.6 8.3 %copy-start = (f32[768,1024]{1,0:T(8,128)S(1)}, f32[768,1024]{1,0:T(8,128)}, u32[]{:S(2)}) copy-start(f32[768,1024]{1,0:T(8,128)} %get-tuple-element.860) | copy-start | bytes 9437188 | tf_op jit(solution)/shard_map/while
  616.5 12.4 %copy-start.1 = (f32[5,32,1024]{2,1,0:T(8,128)}, f32[5,32,1024]{2,1,0:T(8,128)S(1)}, u32[]{:S(2)}) copy-start(f32[5,32,1024]{2,1,0:T(8,128)S(1)} %fusion.377) | copy-start | bytes 1966084 | tf_op jit(solution)/shard_map/while
  631.7 5.7 copy-start.21
  637.4 8.3 %copy-start = (f32[768,1024]{1,0:T(8,128)S(1)}, f32[768,1024]{1,0:T(8,128)}, u32[]{:S(2)}) copy-start(f32[768,1024]{1,0:T(8,128)} %get-tuple-element.860) | copy-start | bytes 9437188 | tf_op jit(solution)/shard_map/while
  673.3 12.4 %copy-start.1 = (f32[5,32,1024]{2,1,0:T(8,128)}, f32[5,32,1024]{2,1,0:T(8,128)S(1)}, u32[]{:S(2)}) copy-start(f32[5,32,1024]{2,1,0:T(8,128)S(1)} %fusion.377) | copy-start | bytes 1966084 | tf_op jit(solution)/shard_map/while
  688.5 5.7 copy-start.21
  694.2 8.3 %copy-start = (f32[768,1024]{1,0:T(8,128)S(1)}, f32[768,1024]{1,0:T(8,128)}, u32[]{:S(2)}) copy-start(f32[768,1024]{1,0:T(8,128)} %get-tuple-element.860) | copy-start | bytes 9437188 | tf_op jit(solution)/shard_map/while
  730.1 12.4 %copy-start.1 = (f32[5,32,1024]{2,1,0:T(8,128)}, f32[5,32,1024]{2,1,0:T(8,128)S(1)}, u32[]{:S(2)}) copy-start(f32[5,32,1024]{2,1,0:T(8,128)S(1)} %fusion.377) | copy-start | bytes 1966084 | tf_op jit(solution)/shard_map/while
  745.3 5.7 copy-start.21
  751.0 8.3 %copy-start = (f32[768,1024]{1,0:T(8,128)S(1)}, f32[768,1024]{1,0:T(8,128)}, u32[]{:S(2)}) copy-start(f32[768,1024]{1,0:T(8,128)} %get-tuple-element.860) | copy-start | bytes 9437188 | tf_op jit(solution)/shard_map/while
  786.9 12.4 %copy-start.1 = (f32[5,32,1024]{2,1,0:T(8,128)}, f32[5,32,1024]{2,1,0:T(8,128)S(1)}, u32[]{:S(2)}) copy-start(f32[5,32,1024]{2,1,0:T(8,128)S(1)} %fusion.377) | copy-start | bytes 1966084 | tf_op jit(solution)/shard_map/while
  802.1 5.7 copy-start.21
  807.8 8.3 %copy-start = (f32[768,1024]{1,0:T(8,128)S(1)}, f32[768,1024]{1,0:T(8,128)}, u32[]{:S(2)}) copy-start(f32[768,1024]{1,0:T(8,128)} %get-tuple-element.860) | copy-start | bytes 9437188 | tf_op jit(solution)/shard_map/while
  (270 other events, 643.7 us)
where the time goes:
time: 840 us; the launch traced here: 824 us
  local copies, waits for them, and re-layouts  471 us (56%)
  other arithmetic  176 us (21%)
  matrix products  145 us (17%)
  starting transfers between devices  18.5 us (2%)
  loops' own time  11 us (1%)
    dot_general x24, matrix products, prolong(): jnp.dot(stacked.reshape(channels * 2 * edge_cells, 3 * plane_size), expan...  105 us
    while x180, other arithmetic  37.7 us
    select_n x24, other arithmetic, minmod(): jnp.where(first_diff * second_diff > 0.0, jnp.sign(first_diff) * jnp.mini...  28.7 us
    dynamic_slice x24, local copies, waits for them, and re-layouts, local(): lax.map(make_indicator(ones_table, expand_table), (primitives, adjoint, g...  26.8 us
    select_n x36, other arithmetic, face_flux(): jnp.where(from_left, wall_flux(left_state[4], normal_axis), jnp.where(fro...  26.7 us
    reshape x12, local copies, waits for them, and re-layouts, residual(): jnp.repeat(flux_top, size_fine, axis=2)  25 us
    concatenate x48, local copies, waits for them, and re-layouts, prolong(): jnp.concatenate([first_term, jnp.repeat(slopes[1], 2, axis=1), jnp.repeat...  21.4 us
    while x636, local copies, waits for them, and re-layouts  21.2 us
  transfers between devices with their start and end apart: 4, of which 1 were waited for; matrix products, arithmetic and copies ran while one was open for 12% of the time, Pallas kernels for 0%

commit v1 on v0

v1 whole, which is shorter than its diff:
```python
import functools

import jax
import jax.numpy as jnp
from jax import lax
from jax.experimental import pallas as pl
from jax.experimental.pallas import tpu as pltpu
from jax.sharding import PartitionSpec as P

EDGE = 16
PLANE = EDGE * EDGE
LANES = 128
PACK = 4
FREESTREAM = (1.0, 0.0, 0.0, 0.3, 1.0)
VMEM = pl.BlockSpec(memory_space=pltpu.VMEM)
SMEM = pl.BlockSpec(memory_space=pltpu.SMEM)


def iota(shape, dim):
    return lax.broadcasted_iota(jnp.int32, shape, dim)


def primitive(state):
    density, mom, energy = state[0], state[1:4], state[4]
    root = lax.rsqrt(density)
    inverse = root * root
    vel = [m * inverse for m in mom]
    square = vel[0] * vel[0] + vel[1] * vel[1] + vel[2] * vel[2]
    return [density, *vel, 0.4 * (energy - 0.5 * density * square)]


def faces_kernel(flow_ref, adj_ref, lat_ref, ver_ref):
    blocks = flow_ref.shape[1]
    lane = iota((blocks, LANES), 1)
    slot, spot = lane >> 4, lane & 15

    def layers(ref, c):
        def tile(i, half):
            return ref[c, :, i * PLANE + half * LANES : i * PLANE + (half + 1) * LANES]

        out = {}
        for half in range(2):
            out[0, half] = tile(0, half)
            out[1, half] = tile(EDGE - 1, half)
            low_j = high_j = low_k = high_k = jnp.zeros((blocks, LANES), jnp.float32)
            for i in range(EDGE):
                if i // 8 == half:
                    il = i % 8
                    low_j = jnp.where(slot == il, pltpu.roll(tile(i, 0), il * 16, 1), low_j)
                    high_j = jnp.where(
                        slot == il, pltpu.roll(tile(i, 1), (il * 16 + 16) % LANES, 1), high_j
                    )
                here = tile(i, half)
                low_k = jnp.where(spot == i, pltpu.roll(here, i, 1), low_k)
                high_k = jnp.where(spot == i, pltpu.roll(here, (LANES + i - 15) % LANES, 1), high_k)
            out[2, half], out[3, half], out[4, half], out[5, half] = low_j, high_j, low_k, high_k
        return out

    def put(face, half, c, value):
        where = slice(half * LANES, (half + 1) * LANES)
        if face < 4:
            lat_ref[face, c, :, where] = value
        else:
            ver_ref[face - 4, c, :, where] = value

    for c in range(5):
        for (face, half), value in layers(flow_ref, c).items():
            put(face, half, c, value)
        for (face, half), value in layers(adj_ref, c).items():
            put(face, half, 5 + c, value)
    for half in range(2):
        where = slice(half * LANES, (half + 1) * LANES)
        for ref, count in ((lat_ref, 4), (ver_ref, 2)):
            for face in range(count):
                prim = primitive([ref[face, c, :, where] for c in range(5)])
                for c in range(1, 5):
                    ref[face, c, :, where] = prim[c]


def gather_kernel(index_ref, lat_ref, out_ref):
    def one(r, carry):
        code = index_ref[r]
        face, block = code & 3, code >> 2
        for c in range(10):
            out_ref[pl.ds(r * 10 + c, 1), :] = lat_ref[face, c, pl.ds(block, 1), :]
        return carry

    lax.fori_loop(0, index_ref.shape[0], one, 0)


def minmod(a, b):
    return jnp.where(a * b > 0.0, jnp.where(jnp.abs(a) < jnp.abs(b), a, b), 0.0)


def derive(state):
    rho, u, v, w, p = state
    inv_root = lax.rsqrt(rho)
    root = rho * inv_root
    enth = (3.5 * p) * (inv_root * inv_root) + 0.5 * (u * u + v * v + w * w)
    return (rho, (u, v, w), p, enth, root, (root * u, root * v, root * w), root * enth)


def roe(left, right, n):
    rho_l, vel_l, p_l, h_l, root_l, rv_l, rh_l = left
    rho_r, vel_r, p_r, h_r, root_r, rv_r, rh_r = right
    t1, t2 = [a for a in range(3) if a != n]
    r = lax.rsqrt(root_l + root_r)
    inv = r * r
    vel = [(a + b) * inv for a, b in zip(rv_l, rv_r)]
    enth = (rh_l + rh_r) * inv
    half_sq = 0.5 * (vel[0] * vel[0] + vel[1] * vel[1] + vel[2] * vel[2])
    c_sq = 0.4 * (enth - half_sq)
    inv_c = lax.rsqrt(c_sq)
    c = c_sq * inv_c
    inv_c_sq = inv_c * inv_c
    rho = root_l * root_r
    un = vel[n]
    dp = p_r - p_l
    scaled = dp * inv_c_sq
    half = 0.5 * scaled
    jump = (0.5 * (rho * inv_c)) * (vel_r[n] - vel_l[n])
    spread, tenth, factor = 0.2 * c, 0.1 * c, 2.5 * inv_c

    def rate(x):
        x = jnp.abs(x)
        return jnp.where(x < spread, x * x * factor + tenth, x)

    slow = rate(un - c) * (half - jump)
    fast = rate(un + c) * (half + jump)
    speed = jnp.abs(un)
    mid = speed * ((rho_r - rho_l) - scaled)
    shear = speed * rho
    both = slow + fast
    diff = c * (fast - slow)
    mass = both + mid
    s1 = shear * (vel_r[t1] - vel_l[t1])
    s2 = shear * (vel_r[t2] - vel_l[t2])
    m_l, m_r = rho_l * vel_l[n], rho_r * vel_r[n]
    out = [None] * 5
    out[0] = m_l + m_r - mass
    out[1 + n] = m_l * vel_l[n] + m_r * vel_r[n] + (p_l + p_r) - (un * mass + diff)
    out[1 + t1] = m_l * vel_l[t1] + m_r * vel_r[t1] - (vel[t1] * mass + s1)
    out[1 + t2] = m_l * vel_l[t2] + m_r * vel_r[t2] - (vel[t2] * mass + s2)
    out[4] = (
        m_l * h_l + m_r * h_r
        - (enth * both + un * diff + mid * half_sq + vel[t1] * s1 + vel[t2] * s2)
    )
    return out


def quads(base, q1, q2):
    low = [b - q for b, q in zip(base, q1)]
    high = [b + q for b, q in zip(base, q1)]
    return [
        derive([b - q for b, q in zip(low, q2)]),
        derive([b + q for b, q in zip(low, q2)]),
        derive([b - q for b, q in zip(high, q2)]),
        derive([b + q for b, q in zip(high, q2)]),
    ]


def moments(lefts, rights, n):
    f = [roe(a, b, n) for a, b in zip(lefts, rights)]
    zero, first, second = [], [], []
    for c in range(5):
        low, high = f[0][c] + f[1][c], f[2][c] + f[3][c]
        zero.append(low + high)
        first.append(high - low)
        second.append((f[1][c] - f[0][c]) + (f[3][c] - f[2][c]))
    return zero + first + second


def dot(a, b):
    total = a[0] * b[0]
    for x, y in zip(a[1:], b[1:]):
        total = total + x * y
    return total


def main_kernel(
    row_ref, slot_ref, edge_ref,
    flow_ref, adj_ref, flag_ref, code_ref, ret_ref, low_ref, high_ref,
    out_ref,
    val, slope, solid, ghost, low_k, low_j, mom_k, mom_j, mom_i, lo_solid,
):
    blocks = flow_ref.shape[1]
    groups = blocks // PACK
    lane = iota((8, LANES), 1)
    row = iota((8, LANES), 0)
    top = row < PACK
    slot, spot = lane >> 4, lane & 15

    def pack(parts):
        tiles = []
        for g in range(groups):
            at = g * PACK % 8
            first, second = parts[g * PACK // 8]
            if first.shape[0] == PACK:
                tiles.append(jnp.concatenate([first, second], axis=0))
            elif at == 0:
                tiles.append(jnp.where(top, first, pltpu.roll(second, 4, 0)))
            else:
                tiles.append(jnp.where(top, pltpu.roll(first, 4, 0), second))
        return tiles

    def read(load, i):
        parts = []
        for start in range(0, blocks, 8):
            rows = slice(start, min(start + 8, blocks))
            parts.append(
                [load(rows, pl.ds(pl.multiple_of(i * PLANE + h * LANES, LANES), LANES)) for h in range(2)]
            )
        return pack(parts)

    def load_layer(i, carry):
        flow = [read(lambda r, s: flow_ref[c, r, s], i) for c in range(5)]
        for g in range(groups):
            for c, x in enumerate(primitive([f[g] for f in flow])):
                val[g, c, 1 + i] = x
        for c in range(5):
            for g, x in enumerate(read(lambda r, s: adj_ref[c, r, s], i)):
                val[g, 5 + c, 1 + i] = x
        for g, x in enumerate(read(lambda r, s: flag_ref[r, s], i)):
            solid[g, 1 + i] = x.astype(jnp.float32)
        return carry

    lax.fori_loop(0, EDGE, load_layer, 0)

    def load_ghost(c, carry):
        for b in range(blocks):
            g, at = b // PACK, b % PACK
            for f in range(6):
                if f < 4:
                    x = ret_ref[pl.ds(row_ref[b * 4 + f] * 10 + c, 1), :]
                else:
                    ref = low_ref if f == 4 else high_ref
                    x = ref[c, pl.ds(slot_ref[b * 2 + f - 4], 1), :]
                ghost[g, f, c, at : at + 1, :] = x[:, :LANES]
                ghost[g, f, c, PACK + at : PACK + at + 1, :] = x[:, LANES:]
        return carry

    lax.fori_loop(0, 10, load_ghost, 0)
    upper_half = 1 - (row >> 2)
    for g in range(groups):
        for f in range(6):
            code = code_ref[f, g]
            half = 1 - upper_half
            own = (code == 4) | ((code >> 1) == half)
            quarter = ((4 * half + (slot >> 1)) << 4) + ((code & 1) << 3) + (spot >> 1)
            index = jnp.where(code == 4, lane, quarter)
            for c in range(10):
                x = ghost[g, f, c]
                x = jnp.where(own, x, pltpu.roll(x, 4, 0))
                x = jnp.take_along_axis(x, index, axis=1, mode="promise_in_bounds")
                if f >= 4:
                    far = FREESTREAM[c] if c < 5 else 0.0
                    x = jnp.where(edge_ref[f - 4] == 1, far, x)
                ghost[g, f, c] = x
    for g in range(groups):
        nothing = jnp.zeros((8, LANES), jnp.float32)
        solid[g, 0] = nothing
        solid[g, EDGE + 1] = nothing
        for c in range(10):
            val[g, c, 0] = ghost[g, 0, c]
            val[g, c, EDGE + 1] = ghost[g, 1, c]
    for d in range(3):
        for c in range(5):
            nothing = jnp.zeros((8, LANES), jnp.float32)
            slope[d, c, 0] = nothing
            slope[d, c, EDGE + 1] = nothing

    def next_k(x, edge, i):
        edge = 0.0 if edge is None else pltpu.roll(edge, 15 - i, 1)
        return jnp.where(spot == 15, edge, pltpu.roll(x, LANES - 1, 1))

    def prev_k(x, edge, i):
        edge = 0.0 if edge is None else pltpu.roll(edge, (LANES - i) % LANES, 1)
        return jnp.where(spot == 0, edge, pltpu.roll(x, 1, 1))

    def place(edge, i, lane_at, upper):
        if edge is None:
            return 0.0
        edge = pltpu.roll(edge, (2 * LANES + lane_at - (i & 7) * 16) % LANES, 1)
        same = (i >> 3) == (1 if upper else 0)
        return jnp.where(same, edge, pltpu.roll(edge, 4, 0))

    def next_j(x, edge, i):
        y = pltpu.roll(x, LANES - 16, 1)
        z = jnp.where(top, pltpu.roll(y, 4, 0), place(edge, i, LANES - 16, True))
        return jnp.where(slot == 7, z, y)

    def prev_j(x, edge, i):
        y = pltpu.roll(x, 16, 1)
        z = jnp.where(top, place(edge, i, 0, False), pltpu.roll(y, 4, 0))
        return jnp.where(slot == 0, z, y)

    def group(g, carry):
        def slopes(i, inner):
            at_k = spot == i
            at_j = ((row >> 2) == (i >> 3)) & (slot == (i & 7))
            for c in range(10):
                own = val[g, c, 1 + i]
                found = [
                    minmod(val[g, c, 2 + i] - own, own - val[g, c, i]),
                    minmod(next_j(own, ghost[g, 3, c], i) - own, own - prev_j(own, ghost[g, 2, c], i)),
                    minmod(next_k(own, ghost[g, 5, c], i) - own, own - prev_k(own, ghost[g, 4, c], i)),
                ]
                found = [0.25 * s for s in found]
                for d in range(3):
                    slope[d, c, 1 + i] = found[d]
                if c < 5:
                    for d, x in enumerate([own, *found]):
                        low_k[d, c] = jnp.where(at_k, pltpu.roll(x, i, 1), low_k[d, c])
                        x = jnp.where(top, x, pltpu.roll(x, 4, 0))
                        low_j[d, c] = jnp.where(at_j, pltpu.roll(x, (i & 7) * 16, 1), low_j[d, c])
            return inner

        lax.fori_loop(0, EDGE, slopes, 0)

        def first_faces(n, lower, cell):
            t1, t2 = [a for a in range(3) if a != n]
            left = derive(lower)
            base = [cell(0, c) - cell(1 + n, c) for c in range(5)]
            rights = quads(base, [cell(1 + t1, c) for c in range(5)], [cell(1 + t2, c) for c in range(5)])
            return moments([left] * 4, rights, n)

        for ref, n in ((mom_j, 1), (mom_k, 2)):
            source = low_j if n == 1 else low_k
            found = first_faces(n, [ghost[g, 2 * n, c] for c in range(5)], lambda d, c: source[d, c])
            for c in range(15):
                ref[c] = found[c]
        found = first_faces(
            0,
            [ghost[g, 0, c] for c in range(5)],
            lambda d, c: val[g, c, 1] if d == 0 else slope[d - 1, c, 1],
        )
        for c in range(15):
            mom_i[c] = found[c]

        def layer(i, inner):
            v = [val[g, c, 1 + i] for c in range(5)]
            q = [[slope[d, c, 1 + i] for c in range(5)] for d in range(3)]
            av = [val[g, 5 + c, 1 + i] for c in range(5)]
            aq = [[slope[d, 5 + c, 1 + i] for c in range(5)] for d in range(3)]
            child = {}
            for a in range(2):
                base = [x + y if a else x - y for x, y in zip(v, q[0])]
                for at, state in enumerate(quads(base, q[1], q[2])):
                    child[a, at >> 1, at & 1] = state

            def side(n, high):
                order = [(s, t) for s in range(2) for t in range(2)]
                return [child[tuple([*st[:n], high, *st[n:]])] for st in order]

            own_solid = solid[g, 1 + i]
            total = jnp.zeros((8, LANES), jnp.float32)
            for n in range(3):
                t1, t2 = [a for a in range(3) if a != n]
                f = [roe(a, b, n) for a, b in zip(side(n, 0), side(n, 1))]
                inside = [(f[0][c] + f[1][c]) + (f[2][c] + f[3][c]) for c in range(5)]
                total = total - 2.0 * dot(aq[n], inside)
                if n == 0:
                    base = [val[g, c, 2 + i] - slope[0, c, 2 + i] for c in range(5)]
                    q1 = [slope[1, c, 2 + i] for c in range(5)]
                    q2 = [slope[2, c, 2 + i] for c in range(5)]
                    up_solid, down_solid = solid[g, 2 + i], solid[g, i]
                else:
                    ahead, behind = (next_j, prev_j) if n == 1 else (next_k, prev_k)
                    base = [ahead(v[c] - q[n][c], ghost[g, 2 * n + 1, c], i) for c in range(5)]
                    q1 = [ahead(q[t1][c], None, i) for c in range(5)]
                    q2 = [ahead(q[t2][c], None, i) for c in range(5)]
                    up_solid, down_solid = ahead(own_solid, None, i), behind(own_solid, None, i)
                above = moments(side(n, 1), quads(base, q1, q2), n)
                if n == 0:
                    below = [mom_i[c] for c in range(15)]
                    for c in range(15):
                        mom_i[c] = above[c]
                else:
                    first = mom_j if n == 1 else mom_k
                    below = [behind(above[c], first[c], i) for c in range(15)]
                outer = [x + y for x, y in zip(av, aq[n])]
                inner_side = [x - y for x, y in zip(av, aq[n])]
                upper = dot([*outer, *aq[t1], *aq[t2]], above)
                lower = dot([*inner_side, *aq[t1], *aq[t2]], below)
                cross = aq[t1][1 + n] * q[t1][4] + aq[t2][1 + n] * q[t2][4]
                wall_up = 8.0 * (outer[1 + n] * (v[4] + q[n][4]) + cross)
                wall_down = 8.0 * (inner_side[1 + n] * (v[4] - q[n][4]) + cross)
                total = total + (
                    jnp.where(up_solid > 0.5, wall_up, upper)
                    - jnp.where(down_solid > 0.5, wall_down, lower)
                )
            total = jnp.where(own_solid > 0.5, 0.0, 0.5 * jnp.abs(total))
            lo_solid[g, i] = total
            return inner

        lax.fori_loop(0, EDGE, layer, 0)
        return carry

    lax.fori_loop(0, groups, group, 0)

    def store(i, carry):
        for g in range(groups):
            x = lo_solid[g, i]
            for h in range(2):
                out_ref[
                    g * PACK : (g + 1) * PACK,
                    pl.ds(pl.multiple_of(i * PLANE + h * LANES, LANES), LANES),
                ] = x[h * PACK : (h + 1) * PACK]
        return carry

    lax.fori_loop(0, EDGE, store, 0)


def local(flow, adjoint, cut_flag, lateral_owner, lateral_link, vertical_link):
    blocks = flow.shape[0]
    groups = blocks // PACK
    peers = lax.axis_size("blk")
    capacity = max(2, 6 * blocks // peers)
    flow_t = jnp.transpose(flow, (1, 0, 2))
    adj_t = jnp.transpose(adjoint, (1, 0, 2))
    f32 = functools.partial(jax.ShapeDtypeStruct, dtype=jnp.float32)

    owners = lateral_owner[:, :, 0].reshape(-1)
    links = lateral_link.reshape(-1)
    count = blocks * 4
    order = jnp.arange(count, dtype=jnp.int32)
    wanted_face = links // 5 * 4 + ((order % 4) ^ 1)
    earlier = (owners[None, :] == owners[:, None]) & (order[None, :] < order[:, None])
    position = jnp.sum(earlier.astype(jnp.int32), axis=1)
    place = owners * capacity + position
    hit = place[None, :] == jnp.arange(peers * capacity, dtype=jnp.int32)[:, None]
    requests = jnp.sum(jnp.where(hit, wanted_face[None, :], 0), axis=1).reshape(peers, capacity)
    wanted = lax.all_to_all(requests, "blk", split_axis=0, concat_axis=0, tiled=True).reshape(-1)

    lateral, vertical = pl.pallas_call(
        faces_kernel,
        out_shape=(f32((4, 10, blocks, PLANE)), f32((2, 10, blocks, PLANE))),
        in_specs=[VMEM, VMEM],
        out_specs=(VMEM, VMEM),
        name="faces",
    )(flow_t, adj_t)

    regions = lax.axis_size("grp")
    region = lax.axis_index("grp")
    from_low = lax.ppermute(vertical[1], "grp", [(r, r + 1) for r in range(regions - 1)])
    from_high = lax.ppermute(vertical[0], "grp", [(r + 1, r) for r in range(regions - 1)])

    replies = pl.pallas_call(
        gather_kernel,
        out_shape=f32((peers * capacity * 10, PLANE)),
        in_specs=[SMEM, VMEM],
        out_specs=VMEM,
        name="gather",
    )(wanted, lateral)
    returned = lax.all_to_all(
        replies.reshape(peers, capacity * 10, PLANE), "blk", split_axis=0, concat_axis=0, tiled=True
    ).reshape(peers * capacity * 10, PLANE)

    ver_code = vertical_link % 5
    ver_code = jnp.where(ver_code == 4, 4, ver_code % 2 * 2 + ver_code // 2)
    codes = jnp.concatenate([lateral_link % 5, ver_code], axis=1)
    codes = codes.reshape(groups, 1, PACK, 6).transpose(3, 0, 1, 2)
    codes = jnp.broadcast_to(codes, (6, groups, 2, PACK)).reshape(6, groups, 8, 1)
    codes = jnp.broadcast_to(codes, (6, groups, 8, LANES))
    edges = jnp.stack([region == 0, region == regions - 1]).astype(jnp.int32)

    tile = functools.partial(pltpu.VMEM, dtype=jnp.float32)
    return pl.pallas_call(
        main_kernel,
        out_shape=f32((blocks, EDGE * PLANE)),
        in_specs=[SMEM] * 3 + [VMEM] * 7,
        out_specs=VMEM,
        scratch_shapes=[
            tile((groups, 10, EDGE + 2, 8, LANES)),
            tile((3, 10, EDGE + 2, 8, LANES)),
            tile((groups, EDGE + 2, 8, LANES)),
            tile((groups, 6, 10, 8, LANES)),
            tile((4, 5, 8, LANES)),
            tile((4, 5, 8, LANES)),
            tile((15, 8, LANES)),
            tile((15, 8, LANES)),
            tile((15, 8, LANES)),
            tile((groups, EDGE, 8, LANES)),
        ],
        compiler_params=pltpu.CompilerParams(vmem_limit_bytes=50 * 1024 * 1024),
        name="indicator",
    )(
        place, (vertical_link // 5).reshape(-1), edges,
        flow_t, adj_t, cut_flag, codes, returned, from_low, from_high,
    )


def solution(mesh):
    spec3 = P(("blk", "grp"), None, None)
    spec2 = P(("blk", "grp"), None)
    return jax.shard_map(
        local,
        mesh=mesh,
        in_specs=(spec3, spec3, spec2, spec3, spec2, spec2),
        out_specs=spec2,
        check_vma=False,
    )
```

time: 840 us -> 96 us (0.11)
  the two profiles are of different devices: /device:TPU:14 before, /device:TPU:0 now
where the time goes in v1:
time: 96 us; the launch traced here: 95.5 us
  Pallas kernels  52.5 us (55%)
  waiting for transfers between devices  17.7 us (18%)
  starting transfers between devices  14.2 us (15%)
  local copies, waits for them, and re-layouts  8.55 us (9%)
  other arithmetic  2.45 us (3%)
    pallas_call x1, Pallas kernels, local(): pl.pallas_call(main_kernel, out_shape=f32((blocks, EDGE * PLANE)), in_spe...  44.1 us
    all_to_all x1, waiting for transfers between devices, local(): lax.all_to_all(replies.reshape(peers, capacity * 10, PLANE), 'blk', split...  15.9 us
    all_to_all x1, starting transfers between devices, local(): lax.all_to_all(requests, 'blk', split_axis=0, concat_axis=0, tiled=True)  7.28 us
    pallas_call x1, Pallas kernels, local(): pl.pallas_call(faces_kernel, out_shape=(f32((4, 10, blocks, PLANE)), f32(...  4.64 us
    all_to_all x1, starting transfers between devices, local(): lax.all_to_all(replies.reshape(peers, capacity * 10, PLANE), 'blk', split...  4.36 us
    pallas_call x1, Pallas kernels, local(): pl.pallas_call(gather_kernel, out_shape=f32((peers * capacity * 10, PLANE...  3.71 us
    reshape x1, local copies, waits for them, and re-layouts, local(): replies.reshape(peers, capacity * 10, PLANE)  2.14 us
  transfers between devices with their start and end apart: 4, of which 2 were waited for; matrix products, arithmetic and copies ran while one was open for 3% of the time, Pallas kernels for 5%

profile of v1, /device:TPU:0, one launch (start us, length us, event | category | flops | bytes accessed | tf_op | source)
XLA Modules:
  0.0 95.5 jit_solution(7272145168790899529)
XLA Ops:
  0.0 0.7 broadcast_divide_fusion
  0.7 0.7 fusion.1
  1.4 0.8 copy.26
  2.2 0.1 reshape_squeeze.3
  2.2 0.2 convert_reduce_fusion
  2.4 0.1 copy.31
  2.5 0.1 div.32
  2.6 0.1 copy.30
  2.7 0.1 and.54
  2.8 0.1 select_reduce_fusion
  2.9 0.7 all_to_all.9
  3.6 7.3 %all-to-all-start = ((s32[8,1,9]{2,1,0:T(1,128)}), s32[8,1,9]{2,1,0:T(1,128)S(1)}, u32[]{:S(2)}, u32[]{:S(2)}) async-start(s32[8,1,9]{2,1,0:T(1,128)} %bitcast.7), calls=%async_computation | async-start | bytes 8192 | tf_op jit(solution)/shard_map/all_to_all | solution.py:433
  10.9 4.6 %faces.1 = (f32[4,10,12,256]{3,2,1,0:T(8,128)}, f32[2,10,12,256]{3,2,1,0:T(8,128)}) custom-call(f32[5,12,4096]{2,1,0:T(8,128)} %bitcast.15, f32[5,12,4096]{2,1,0:T(8,128)} %bitcast.17), custom_call_target="tpu_custom_call" | custom-call | tf_op jit(solution)/shard_map/faces/pallas_call | solution.py:435
  15.5 1.8 %all-to-all-done = s32[8,1,9]{2,1,0:T(1,128)S(1)} async-done(((s32[8,1,9]{2,1,0:T(1,128)}), s32[8,1,9]{2,1,0:T(1,128)S(1)}, u32[]{:S(2)}, u32[]{:S(2)}) %all-to-all-start) | async-done | bytes 320 | tf_op jit(solution)/shard_map/all_to_all | solution.py:433
  17.3 0.5 broadcast.98
  17.8 0.7 reduce.3
  18.5 0.6 reshape.75.index_ref
  19.1 3.7 %gather.1 = f32[720,256]{1,0:T(8,128)} custom-call(s32[72]{0:T(128)} %reshape.75.index_ref, f32[4,10,12,256]{3,2,1,0:T(8,128)} %get-tuple-element.7.lat_ref), custom_call_target="tpu_custom_call" | custom-call | tf_op jit(solution)/shard_map/gather/pallas_call | solution.py:448
  22.8 0.0 copy-start.3
  22.8 2.1 %reshape.76 = f32[8,90,256]{2,1,0:T(8,128)} reshape(f32[720,256]{1,0:T(8,128)} %gather.1) | data formatting | bytes 1474560 | tf_op jit(solution)/shard_map/reshape | solution.py:456
  24.9 0.0 copy-start.4
  24.9 0.0 copy-start.1
  24.9 4.4 %all-to-all-start.1 = ((f32[8,90,256]{2,1,0:T(8,128)}), f32[8,90,256]{2,1,0:T(8,128)}, u32[]{:S(2)}, u32[]{:S(2)}) async-start(f32[8,90,256]{2,1,0:T(8,128)} %reshape.76), calls=%async_computation.1 | async-start | bytes 1572864 | tf_op jit(solution)/shard_map/all_to_all | solution.py:455
  29.3 0.0 copy-start
  29.3 0.0 copy-done.3
  29.3 0.7 slice_bitcast_fusion
  30.1 1.3 %collective-permute-start = (f32[10,12,256]{2,1,0:T(8,128)}, f32[10,12,256]{2,1,0:T(8,128)S(1)}, u32[]{:S(2)}, u32[]{:S(2)}) collective-permute-start(f32[10,12,256]{2,1,0:T(8,128)} %get-tuple-element.10), channel_id=1, source_target_pairs={{0,1},{1,2},{2,3},{4,5},{5,6},{6,7},{8,9},{9,10},{10,11},{12,13},{... | collective-permute-start | bytes 368648 | tf_op jit(solution)/shard_map/ppermute | solution.py:445
  31.4 1.3 %collective-permute-start.1 = (f32[10,12,256]{2,1,0:T(8,128)}, f32[10,12,256]{2,1,0:T(8,128)}, u32[]{:S(2)}, u32[]{:S(2)}) collective-permute-start(f32[10,12,256]{2,1,0:T(8,128)} %get-tuple-element.9), channel_id=1, source_target_pairs={{1,0},{2,1},{3,2},{5,4},{6,5},{7,6},{9,8},{10,9},{11,10},{13,12},{... | collective-permute-start | bytes 368648 | tf_op jit(solution)/shard_map/ppermute | solution.py:446
  32.7 0.0 copy-done.4
  32.7 0.1 copy.28
  32.8 0.1 copy.29
  32.9 0.1 copy.27
  33.0 0.1 reshape.73.slot_ref
  33.1 0.1 add_convert_fusion.edge_ref
  33.2 15.9 %all-to-all-done.1 = f32[8,90,256]{2,1,0:T(8,128)} async-done(((f32[8,90,256]{2,1,0:T(8,128)}), f32[8,90,256]{2,1,0:T(8,128)}, u32[]{:S(2)}, u32[]{:S(2)}) %all-to-all-start.1) | async-done | bytes 737312 | tf_op jit(solution)/shard_map/all_to_all | solution.py:455
  49.1 1.2 %reshape.77.ret_ref = f32[720,256]{1,0:T(8,128)S(1)} reshape(f32[8,90,256]{2,1,0:T(8,128)} %all-to-all-done.1) | data formatting | bytes 1474560 | tf_op jit(solution)/shard_map/reshape | solution.py:457
  50.3 0.0 collective-permute-done.low_ref
  50.3 0.0 collective-permute-done.1.high_ref
  50.3 0.1 broadcast_in_dim.36.code_ref
  50.4 0.0 copy-done.1
  50.4 0.0 copy-done
  50.4 0.0 copy-start.2
  50.4 0.9 copy-done.2
  51.4 44.1 %indicator.1 = f32[12,4096]{1,0:T(8,128)} custom-call(s32[48]{0:T(128)S(1)} %multiply_add_fusion.row_ref, s32[24]{0:T(128)S(1)} %reshape.73.slot_ref, s32[2]{0:T(128)S(1)} %add_convert_fusion.edge_ref, f32[5,12,4096]{2,1,0:T(8,128)S(1)} %bitcast.16, f32[5,12,4096]{2,1,0:T(8,128)S(1)} %bitcast.18, s32[12,4096]{1,0:T(8,128)S(1)} %copy-done.2, ...), custom_call_target="tpu_custom_call" | custom-call | tf_op jit(solution)/shard_map/indicator/pallas_call | solution.py:468
  (6 shorter events, 0.1 us)
Async XLA Ops:
  3.6 13.7 %all-to-all-start = ((s32[8,1,9]{2,1,0:T(1,128)}), s32[8,1,9]{2,1,0:T(1,128)S(1)}, u32[]{:S(2)}, u32[]{:S(2)}) async-start(s32[8,1,9]{2,1,0:T(1,128)} %bitcast.7), calls=%async_computation | async-start | bytes 8192 | tf_op jit(solution)/shard_map/all_to_all | solution.py:433
  22.8 6.5 %copy-start.3 = (f32[2,10,12,256]{3,2,1,0:T(8,128)S(1)}, f32[2,10,12,256]{3,2,1,0:T(8,128)}, u32[]{:S(2)}) copy-start(f32[2,10,12,256]{3,2,1,0:T(8,128)} %get-tuple-element.8) | copy-start | bytes 737284
  24.9 7.7 %copy-start.4 = (s32[12,2]{0,1:T(2,128)S(1)}, s32[12,2]{0,1:T(2,128)}, u32[]{:S(2)}) copy-start(s32[12,2]{0,1:T(2,128)} %param.11) | copy-start | bytes 292
  24.9 25.5 %copy-start.1 = (f32[12,5,4096]{2,0,1:T(8,128)S(1)}, f32[12,5,4096]{2,0,1:T(8,128)}, u32[]{:S(2)}) copy-start(f32[12,5,4096]{2,0,1:T(8,128)} %param.7) | copy-start | bytes 2949124
  24.9 24.1 %all-to-all-start.1 = ((f32[8,90,256]{2,1,0:T(8,128)}), f32[8,90,256]{2,1,0:T(8,128)}, u32[]{:S(2)}, u32[]{:S(2)}) async-start(f32[8,90,256]{2,1,0:T(8,128)} %reshape.76), calls=%async_computation.1 | async-start | bytes 1572864 | tf_op jit(solution)/shard_map/all_to_all | solution.py:455
  29.3 21.1 %copy-start = (f32[12,5,4096]{2,0,1:T(8,128)S(1)}, f32[12,5,4096]{2,0,1:T(8,128)}, u32[]{:S(2)}) copy-start(f32[12,5,4096]{2,0,1:T(8,128)} %param.6) | copy-start | bytes 2949124
  30.1 20.2 %collective-permute-start = (f32[10,12,256]{2,1,0:T(8,128)}, f32[10,12,256]{2,1,0:T(8,128)S(1)}, u32[]{:S(2)}, u32[]{:S(2)}) collective-permute-start(f32[10,12,256]{2,1,0:T(8,128)} %get-tuple-element.10), channel_id=1, source_target_pairs={{0,1},{1,2},{2,3},{4,5},{5,6},{6,7},{8,9},{9,10},{10,11},{12,13},{... | collective-permute-start | bytes 368648 | tf_op jit(solution)/shard_map/ppermute | solution.py:445
  31.4 19.0 %collective-permute-start.1 = (f32[10,12,256]{2,1,0:T(8,128)}, f32[10,12,256]{2,1,0:T(8,128)}, u32[]{:S(2)}, u32[]{:S(2)}) collective-permute-start(f32[10,12,256]{2,1,0:T(8,128)} %get-tuple-element.9), channel_id=1, source_target_pairs={{1,0},{2,1},{3,2},{5,4},{6,5},{7,6},{9,8},{10,9},{11,10},{13,12},{... | collective-permute-start | bytes 368648 | tf_op jit(solution)/shard_map/ppermute | solution.py:446
  50.4 1.0 copy-start.2

commit v2 on v1

--- a/solution.py
+++ b/solution.py
@@ -14,6 +14,7 @@
 FREESTREAM = (1.0, 0.0, 0.0, 0.3, 1.0)
 VMEM = pl.BlockSpec(memory_space=pltpu.VMEM)
 SMEM = pl.BlockSpec(memory_space=pltpu.SMEM)
+MESH = pl.DeviceIdType.MESH
 
 
 def iota(shape, dim):
@@ -29,8 +30,29 @@
     return [density, *vel, 0.4 * (energy - 0.5 * density * square)]
 
 
-def faces_kernel(flow_ref, adj_ref, lat_ref, ver_ref):
+def faces_kernel(req_ref, flow_ref, adj_ref, lat_ref, ver_ref, want_ref, send_sem, recv_sem, own_sem):
     blocks = flow_ref.shape[1]
+    peers = req_ref.shape[0]
+    me = lax.axis_index("blk")
+
+    def copy(d):
+        peer = lax.rem(me + d, peers)
+        return pltpu.make_async_remote_copy(
+            src_ref=req_ref.at[peer],
+            dst_ref=want_ref.at[me],
+            send_sem=send_sem.at[d],
+            recv_sem=recv_sem.at[d],
+            device_id={"blk": peer},
+            device_id_type=MESH,
+        )
+
+    barrier = pltpu.get_barrier_semaphore()
+    for d in range(1, peers):
+        pl.semaphore_signal(
+            barrier, inc=1, device_id={"blk": lax.rem(me + d, peers)}, device_id_type=MESH
+        )
+    own = pltpu.make_async_copy(req_ref.at[me], want_ref.at[me], own_sem)
+    own.start()
     lane = iota((blocks, LANES), 1)
     slot, spot = lane >> 4, lane & 15
 
@@ -64,6 +86,10 @@
             ver_ref[face - 4, c, :, where] = value
 
     for c in range(5):
+        if c == 3:
+            pl.semaphore_wait(barrier, peers - 1)
+            for d in range(1, peers):
+                copy(d).start()
         for (face, half), value in layers(flow_ref, c).items():
             put(face, half, c, value)
         for (face, half), value in layers(adj_ref, c).items():
@@ -75,17 +101,140 @@
                 prim = primitive([ref[face, c, :, where] for c in range(5)])
                 for c in range(1, 5):
                     ref[face, c, :, where] = prim[c]
-
-
-def gather_kernel(index_ref, lat_ref, out_ref):
-    def one(r, carry):
-        code = index_ref[r]
-        face, block = code & 3, code >> 2
+    own.wait()
+    for d in range(1, peers):
+        copy(d).wait()
+
+
+def plan_kernel(capacity, owner_ref, link_ref, req_ref, place_ref, count_ref):
+    def clear(p, carry):
+        count_ref[p] = 0
+        for s in range(capacity):
+            req_ref[p, 0, s] = 0
+        return carry
+
+    lax.fori_loop(0, req_ref.shape[0], clear, 0)
+
+    def ask(b, carry):
+        for f in range(4):
+            owner = owner_ref[f, 0, b]
+            at = count_ref[owner]
+            count_ref[owner] = at + 1
+            req_ref[owner, 0, at] = link_ref[f, b] // 5 * 4 + (f ^ 1)
+            place_ref[b * 4 + f] = owner * 4096 + at
+        return carry
+
+    lax.fori_loop(0, link_ref.shape[1], ask, 0)
+
+
+def exchange_kernel(
+    capacity, want_ref, lat_ref, ver_ref, ret_ref, low_ref, high_ref,
+    stage, send_sem, recv_sem, up_sem, down_sem,
+):
+    peers = ret_ref.shape[0]
+    me = lax.axis_index("blk")
+    region = lax.axis_index("grp")
+    last = lax.axis_size("grp") - 1
+    has_low, has_high = region > 0, region < last
+
+    def copy(d):
+        peer = lax.rem(me + d, peers)
+        return pltpu.make_async_remote_copy(
+            src_ref=stage.at[peer],
+            dst_ref=ret_ref.at[me],
+            send_sem=send_sem.at[d],
+            recv_sem=recv_sem.at[d],
+            device_id={"blk": peer},
+            device_id_type=MESH,
+        )
+
+    def vertical(source, target, sem, step):
+        return pltpu.make_async_remote_copy(
+            src_ref=ver_ref.at[source],
+            dst_ref=target,
+            send_sem=sem.at[0],
+            recv_sem=sem.at[1],
+            device_id={"grp": region + step},
+            device_id_type=MESH,
+        )
+
+    upward = vertical(1, low_ref, up_sem, 1)
+    downward = vertical(0, high_ref, down_sem, -1)
+    barrier = pltpu.get_barrier_semaphore()
+    for d in range(1, peers):
+        pl.semaphore_signal(
+            barrier, inc=1, device_id={"blk": lax.rem(me + d, peers)}, device_id_type=MESH
+        )
+    for there, step in ((has_low, -1), (has_high, 1)):
+        @pl.when(there)
+        def _():
+            pl.semaphore_signal(
+                barrier, inc=1, device_id={"grp": region + step}, device_id_type=MESH
+            )
+
+    def gather(peer, ref, at):
+        def one(s, carry):
+            code = want_ref[peer, 0, s]
+            face, block = code & 3, code >> 2
+            for c in range(10):
+                ref[at, pl.ds(s * 10 + c, 1), :] = lat_ref[face, c, pl.ds(block, 1), :]
+            return carry
+
+        lax.fori_loop(0, capacity, one, 0)
+
+    def fill(d):
+        peer = lax.rem(me + d, peers)
+        gather(peer, stage, peer)
+
+    fill(1)
+    pl.semaphore_wait(
+        barrier, peers - 1 + has_low.astype(jnp.int32) + has_high.astype(jnp.int32)
+    )
+
+    def send(d, carry):
+        fill(d)
+        copy(d - 1).start()
+        return carry
+
+    lax.fori_loop(2, peers, send, 0)
+    gather(me, ret_ref, me)
+    copy(peers - 1).start()
+
+    @pl.when(has_high)
+    def _():
+        upward.start()
+
+    @pl.when(has_low)
+    def _():
+        downward.start()
+
+    def far(ref):
         for c in range(10):
-            out_ref[pl.ds(r * 10 + c, 1), :] = lat_ref[face, c, pl.ds(block, 1), :]
-        return carry
-
-    lax.fori_loop(0, index_ref.shape[0], one, 0)
+            ref[c] = jnp.full(ref.shape[1:], FREESTREAM[c] if c < 5 else 0.0, jnp.float32)
+
+    @pl.when(has_low)
+    def _():
+        downward.wait_send()
+        upward.wait_recv()
+
+    @pl.when(jnp.logical_not(has_low))
+    def _():
+        far(low_ref)
+
+    @pl.when(has_high)
+    def _():
+        upward.wait_send()
+        downward.wait_recv()
+
+    @pl.when(jnp.logical_not(has_high))
+    def _():
+        far(high_ref)
+
+    def finish(d, carry):
+        copy(d).wait()
+        return carry
+
+    lax.fori_loop(1, peers, finish, 0)
 
 
 def minmod(a, b):
@@ -178,8 +327,8 @@
 
 
 def main_kernel(
-    row_ref, slot_ref, edge_ref,
-    flow_ref, adj_ref, flag_ref, code_ref, ret_ref, low_ref, high_ref,
+    place_ref, link_ref, ver_link_ref,
+    flow_ref, adj_ref, flag_ref, ret_ref, low_ref, high_ref,
     out_ref,
     val, slope, solid, ghost, low_k, low_j, mom_k, mom_j, mom_i, lo_solid,
 ):
@@ -231,10 +380,11 @@
             g, at = b // PACK, b % PACK
             for f in range(6):
                 if f < 4:
-                    x = ret_ref[pl.ds(row_ref[b * 4 + f] * 10 + c, 1), :]
+                    at_row = place_ref[b * 4 + f]
+                    x = ret_ref[at_row >> 12, pl.ds((at_row & 4095) * 10 + c, 1), :]
                 else:
                     ref = low_ref if f == 4 else high_ref
-                    x = ref[c, pl.ds(slot_ref[b * 2 + f - 4], 1), :]
+                    x = ref[c, pl.ds(ver_link_ref[f - 4, b] // 5, 1), :]
                 ghost[g, f, c, at : at + 1, :] = x[:, :LANES]
                 ghost[g, f, c, PACK + at : PACK + at + 1, :] = x[:, LANES:]
         return carry
@@ -243,7 +393,13 @@
     upper_half = 1 - (row >> 2)
     for g in range(groups):
         for f in range(6):
-            code = code_ref[f, g]
+            code = 0
+            for at in range(PACK):
+                b = g * PACK + at
+                one = lax.rem(link_ref[f, b] if f < 4 else ver_link_ref[f - 4, b], 5)
+                if f >= 4:
+                    one = jnp.where(one == 4, 4, ((one & 1) << 1) + (one >> 1))
+                code = jnp.where((row & 3) == at, one, code)
             half = 1 - upper_half
             own = (code == 4) | ((code >> 1) == half)
             quarter = ((4 * half + (slot >> 1)) << 4) + ((code & 1) << 3) + (spot >> 1)
@@ -252,9 +408,6 @@
                 x = ghost[g, f, c]
                 x = jnp.where(own, x, pltpu.roll(x, 4, 0))
                 x = jnp.take_along_axis(x, index, axis=1, mode="promise_in_bounds")
-                if f >= 4:
-                    far = FREESTREAM[c] if c < 5 else 0.0
-                    x = jnp.where(edge_ref[f - 4] == 1, far, x)
                 ghost[g, f, c] = x
     for g in range(groups):
         nothing = jnp.zeros((8, LANES), jnp.float32)
@@ -420,55 +573,61 @@
     adj_t = jnp.transpose(adjoint, (1, 0, 2))
     f32 = functools.partial(jax.ShapeDtypeStruct, dtype=jnp.float32)
 
-    owners = lateral_owner[:, :, 0].reshape(-1)
-    links = lateral_link.reshape(-1)
-    count = blocks * 4
-    order = jnp.arange(count, dtype=jnp.int32)
-    wanted_face = links // 5 * 4 + ((order % 4) ^ 1)
-    earlier = (owners[None, :] == owners[:, None]) & (order[None, :] < order[:, None])
-    position = jnp.sum(earlier.astype(jnp.int32), axis=1)
-    place = owners * capacity + position
-    hit = place[None, :] == jnp.arange(peers * capacity, dtype=jnp.int32)[:, None]
-    requests = jnp.sum(jnp.where(hit, wanted_face[None, :], 0), axis=1).reshape(peers, capacity)
-    wanted = lax.all_to_all(requests, "blk", split_axis=0, concat_axis=0, tiled=True).reshape(-1)
-
-    lateral, vertical = pl.pallas_call(
+    owner_t = jnp.transpose(lateral_owner, (1, 2, 0))
+    link_t, ver_link_t = lateral_link.T, vertical_link.T
+    i32 = functools.partial(jax.ShapeDtypeStruct, dtype=jnp.int32)
+    requests, place = pl.pallas_call(
+        functools.partial(plan_kernel, capacity),
+        out_shape=(i32((peers, 1, LANES)), i32((blocks * 4,))),
+        in_specs=[SMEM, SMEM],
+        out_specs=(SMEM, SMEM),
+        scratch_shapes=[pltpu.SMEM((peers,), jnp.int32)],
+        name="plan",
+    )(owner_t, link_t)
+
+    lateral, vertical, wanted = pl.pallas_call(
         faces_kernel,
-        out_shape=(f32((4, 10, blocks, PLANE)), f32((2, 10, blocks, PLANE))),
-        in_specs=[VMEM, VMEM],
-        out_specs=(VMEM, VMEM),
+        out_shape=(
+            f32((4, 10, blocks, PLANE)),
+            f32((2, 10, blocks, PLANE)),
+            i32((peers, 1, LANES)),
+        ),
+        in_specs=[VMEM] * 3,
+        out_specs=(VMEM,) * 3,
+        scratch_shapes=[
+            pltpu.SemaphoreType.DMA((peers,)),
+            pltpu.SemaphoreType.DMA((peers,)),
+            pltpu.SemaphoreType.DMA,
+        ],
+        compiler_params=pltpu.CompilerParams(collective_id=0, has_side_effects=True),
         name="faces",
-    )(flow_t, adj_t)
-
-    regions = lax.axis_size("grp")
-    region = lax.axis_index("grp")
-    from_low = lax.ppermute(vertical[1], "grp", [(r, r + 1) for r in range(regions - 1)])
-    from_high = lax.ppermute(vertical[0], "grp", [(r + 1, r) for r in range(regions - 1)])
-
-    replies = pl.pallas_call(
-        gather_kernel,
-        out_shape=f32((peers * capacity * 10, PLANE)),
-        in_specs=[SMEM, VMEM],
-        out_specs=VMEM,
-        name="gather",
-    )(wanted, lateral)
-    returned = lax.all_to_all(
-        replies.reshape(peers, capacity * 10, PLANE), "blk", split_axis=0, concat_axis=0, tiled=True
-    ).reshape(peers * capacity * 10, PLANE)
-
-    ver_code = vertical_link % 5
-    ver_code = jnp.where(ver_code == 4, 4, ver_code % 2 * 2 + ver_code // 2)
-    codes = jnp.concatenate([lateral_link % 5, ver_code], axis=1)
-    codes = codes.reshape(groups, 1, PACK, 6).transpose(3, 0, 1, 2)
-    codes = jnp.broadcast_to(codes, (6, groups, 2, PACK)).reshape(6, groups, 8, 1)
-    codes = jnp.broadcast_to(codes, (6, groups, 8, LANES))
-    edges = jnp.stack([region == 0, region == regions - 1]).astype(jnp.int32)
+    )(requests, flow_t, adj_t)
+
+    returned, from_low, from_high = pl.pallas_call(
+        functools.partial(exchange_kernel, capacity),
+        out_shape=(
+            f32((peers, capacity * 10, PLANE)),
+            f32((10, blocks, PLANE)),
+            f32((10, blocks, PLANE)),
+        ),
+        in_specs=[SMEM, VMEM, VMEM],
+        out_specs=(VMEM,) * 3,
+        scratch_shapes=[
+            pltpu.VMEM((peers, capacity * 10, PLANE), jnp.float32),
+            pltpu.SemaphoreType.DMA((peers,)),
+            pltpu.SemaphoreType.DMA((peers,)),
+            pltpu.SemaphoreType.DMA((2,)),
+            pltpu.SemaphoreType.DMA((2,)),
+        ],
+        compiler_params=pltpu.CompilerParams(collective_id=1, has_side_effects=True),
+        name="exchange",
+    )(wanted, lateral, vertical)
 
     tile = functools.partial(pltpu.VMEM, dtype=jnp.float32)
     return pl.pallas_call(
         main_kernel,
         out_shape=f32((blocks, EDGE * PLANE)),
-        in_specs=[SMEM] * 3 + [VMEM] * 7,
+        in_specs=[SMEM] * 3 + [VMEM] * 6,
         out_specs=VMEM,
         scratch_shapes=[
             tile((groups, 10, EDGE + 2, 8, LANES)),
@@ -485,8 +644,8 @@
         compiler_params=pltpu.CompilerParams(vmem_limit_bytes=50 * 1024 * 1024),
         name="indicator",
     )(
-        place, (vertical_link // 5).reshape(-1), edges,
-        flow_t, adj_t, cut_flag, codes, returned, from_low, from_high,
+        place, link_t, ver_link_t,
+        flow_t, adj_t, cut_flag, returned, from_low, from_high,
     )
 
 

time: 96 us -> 84.6 us (0.88)
  the two profiles are of different devices: /device:TPU:0 before, /device:TPU:14 now
where the time goes in v2:
time: 84.6 us; the launch traced here: 83.4 us
  Pallas kernels  80.3 us (95%)
  local copies, waits for them, and re-layouts  2.99 us (4%)
    pallas_call x1, Pallas kernels, local(): pl.pallas_call(main_kernel, out_shape=f32((blocks, EDGE * PLANE)), in_spe...  45.4 us
    pallas_call x1, Pallas kernels, local(): pl.pallas_call(functools.partial(exchange_kernel, capacity), out_shape=(f...  23.5 us
    pallas_call x1, Pallas kernels, local(): pl.pallas_call(faces_kernel, out_shape=(f32((4, 10, blocks, PLANE)), f32(...  9.52 us
    unnamed x18, local copies, waits for them, and re-layouts  2.99 us
    pallas_call x1, Pallas kernels, local(): pl.pallas_call(functools.partial(plan_kernel, capacity), out_shape=(i32((...  1.96 us

profile of v2, /device:TPU:14, one launch (start us, length us, event | category | flops | bytes accessed | tf_op | source)
XLA Modules:
  0.0 83.4 jit_solution(11220377890054780361)
XLA Ops:
  0.0 2.0 %plan.1 = (s32[8,1,128]{2,1,0:T(1,128)}, s32[48]{0:T(128)}) custom-call(s32[4,1,12]{2,1,0:T(1,128)} %bitcast.12, s32[4,12]{1,0:T(4,128)} %bitcast.9), custom_call_target="tpu_custom_call" | custom-call | tf_op jit(solution)/shard_map/plan/pallas_call | solution.py:579
  2.0 0.0 copy-start
  2.0 0.0 copy-start.1
  2.0 0.0 copy-start.3
  2.0 0.0 copy-start.6
  2.0 0.0 copy-start.7
  2.0 0.0 copy-start.8
  2.0 9.5 %faces.1 = (f32[4,10,12,256]{3,2,1,0:T(8,128)}, f32[2,10,12,256]{3,2,1,0:T(8,128)}, s32[8,1,128]{2,1,0:T(1,128)}) custom-call(s32[8,1,128]{2,1,0:T(1,128)} %get-tuple-element.14.req_ref, f32[5,12,4096]{2,1,0:T(8,128)} %bitcast.5, f32[5,12,4096]{2,1,0:T(8,128)} %bitcast.7), custom_call_target="tpu_custom_call" | custom-call | tf_op jit(solution)/shard_map/faces/pallas_call | solution.py:588
  11.6 23.5 %exchange.1 = (f32[8,90,256]{2,1,0:T(8,128)}, f32[10,12,256]{2,1,0:T(8,128)}, f32[10,12,256]{2,1,0:T(8,128)}) custom-call(s32[8,1,128]{2,1,0:T(1,128)} %get-tuple-element.15.want_ref, f32[4,10,12,256]{3,2,1,0:T(8,128)} %get-tuple-element.16.lat_ref, f32[2,10,12,256]{3,2,1,0:T(8,128)} %get-tuple-element.17.ver_ref), custom_call_target="tpu_custom_call" | custom-call | tf_op jit(solution)/shard_map/exchange/pallas_call | solution.py:606
  35.0 0.0 copy-done
  35.0 0.0 copy-done.1
  35.1 0.0 copy-done.3
  35.1 0.0 copy-done.6
  35.1 0.0 copy-done.7
  35.1 0.0 copy-done.8
  35.1 0.0 copy-start.2
  35.1 1.1 %copy-done.2 = f32[8,90,256]{2,1,0:T(8,128)S(1)} copy-done((f32[8,90,256]{2,1,0:T(8,128)S(1)}, f32[8,90,256]{2,1,0:T(8,128)}, u32[]{:S(2)}) %copy-start.2) | copy-done | bytes 737304
  36.2 0.0 copy-start.4
  36.2 0.9 %copy-done.4 = f32[10,12,256]{2,1,0:T(8,128)S(1)} copy-done((f32[10,12,256]{2,1,0:T(8,128)S(1)}, f32[10,12,256]{2,1,0:T(8,128)}, u32[]{:S(2)}) %copy-start.4) | copy-done | bytes 122904
  37.1 0.0 copy-start.5
  37.1 0.9 %copy-done.5 = f32[10,12,256]{2,1,0:T(8,128)S(1)} copy-done((f32[10,12,256]{2,1,0:T(8,128)S(1)}, f32[10,12,256]{2,1,0:T(8,128)}, u32[]{:S(2)}) %copy-start.5) | copy-done | bytes 122904
  38.1 45.4 %indicator.1 = f32[12,4096]{1,0:T(8,128)} custom-call(s32[48]{0:T(128)S(1)} %copy-done.8, s32[4,12]{1,0:T(4,128)S(1)} %bitcast.10, s32[2,12]{1,0:T(2,128)S(1)} %bitcast.11, f32[5,12,4096]{2,1,0:T(8,128)S(1)} %bitcast.6, f32[5,12,4096]{2,1,0:T(8,128)S(1)} %bitcast.8, s32[12,4096]{1,0:T(8,128)S(1)} %copy-done.3, f32[8,90,256]{2,1,0:T(8,128)S(1)} %copy-done.2, ...), custom_call_target="tpu_custom_call" | custom-call | tf_op jit(solution)/shard_map/indicator/pallas_call | solution.py:627
Async XLA Ops:
  2.0 33.1 %copy-start = (f32[12,5,4096]{2,0,1:T(8,128)S(1)}, f32[12,5,4096]{2,0,1:T(8,128)}, u32[]{:S(2)}) copy-start(f32[12,5,4096]{2,0,1:T(8,128)} %param.6) | copy-start | bytes 2949124
  2.0 33.1 %copy-start.1 = (f32[12,5,4096]{2,0,1:T(8,128)S(1)}, f32[12,5,4096]{2,0,1:T(8,128)}, u32[]{:S(2)}) copy-start(f32[12,5,4096]{2,0,1:T(8,128)} %param.7) | copy-start | bytes 2949124
  2.0 33.1 %copy-start.3 = (s32[12,4096]{1,0:T(8,128)S(1)}, s32[12,4096]{1,0:T(8,128)}, u32[]{:S(2)}) copy-start(s32[12,4096]{1,0:T(8,128)} %flag_ref.1) | copy-start | bytes 589828
  2.0 33.1 %copy-start.6 = (s32[12,4]{0,1:T(4,128)S(1)}, s32[12,4]{0,1:T(4,128)}, u32[]{:S(2)}) copy-start(s32[12,4]{0,1:T(4,128)} %param.10) | copy-start | bytes 580
  2.0 33.1 %copy-start.7 = (s32[12,2]{0,1:T(2,128)S(1)}, s32[12,2]{0,1:T(2,128)}, u32[]{:S(2)}) copy-start(s32[12,2]{0,1:T(2,128)} %param.11) | copy-start | bytes 292
  2.0 33.1 %copy-start.8 = (s32[48]{0:T(128)S(1)}, s32[48]{0:T(128)}, u32[]{:S(2)}) copy-start(s32[48]{0:T(128)} %get-tuple-element.13.place_ref) | copy-start | bytes 580
  35.1 1.1 %copy-start.2 = (f32[8,90,256]{2,1,0:T(8,128)S(1)}, f32[8,90,256]{2,1,0:T(8,128)}, u32[]{:S(2)}) copy-start(f32[8,90,256]{2,1,0:T(8,128)} %get-tuple-element.18.ret_ref) | copy-start | bytes 2211844
  36.2 0.9 %copy-start.4 = (f32[10,12,256]{2,1,0:T(8,128)S(1)}, f32[10,12,256]{2,1,0:T(8,128)}, u32[]{:S(2)}) copy-start(f32[10,12,256]{2,1,0:T(8,128)} %get-tuple-element.19.low_ref) | copy-start | bytes 368644
  37.1 0.9 %copy-start.5 = (f32[10,12,256]{2,1,0:T(8,128)S(1)}, f32[10,12,256]{2,1,0:T(8,128)}, u32[]{:S(2)}) copy-start(f32[10,12,256]{2,1,0:T(8,128)} %get-tuple-element.20.high_ref) | copy-start | bytes 368644

commit v3 on v2

--- a/solution.py
+++ b/solution.py
@@ -14,6 +14,7 @@
 FREESTREAM = (1.0, 0.0, 0.0, 0.3, 1.0)
 VMEM = pl.BlockSpec(memory_space=pltpu.VMEM)
 SMEM = pl.BlockSpec(memory_space=pltpu.SMEM)
+HBM = pl.BlockSpec(memory_space=pltpu.HBM)
 MESH = pl.DeviceIdType.MESH
 
 
@@ -30,18 +31,22 @@
     return [density, *vel, 0.4 * (energy - 0.5 * density * square)]
 
 
-def faces_kernel(req_ref, flow_ref, adj_ref, lat_ref, ver_ref, want_ref, send_sem, recv_sem, own_sem):
+def halo_kernel(
+    capacity, req_ref, flow_ref, adj_ref, ret_ref, low_ref, high_ref,
+    lat_ref, ver_ref, want_ref, index_ref, stage,
+    ask_sem, asked_sem, send_sem, recv_sem, up_sem, down_sem, own_sem,
+):
     blocks = flow_ref.shape[1]
     peers = req_ref.shape[0]
     me = lax.axis_index("blk")
 
-    def copy(d):
+    def request(d):
         peer = lax.rem(me + d, peers)
         return pltpu.make_async_remote_copy(
             src_ref=req_ref.at[peer],
             dst_ref=want_ref.at[me],
-            send_sem=send_sem.at[d],
-            recv_sem=recv_sem.at[d],
+            send_sem=ask_sem.at[d],
+            recv_sem=asked_sem.at[d],
             device_id={"blk": peer},
             device_id_type=MESH,
         )
@@ -51,6 +56,15 @@
         pl.semaphore_signal(
             barrier, inc=1, device_id={"blk": lax.rem(me + d, peers)}, device_id_type=MESH
         )
+    region = lax.axis_index("grp")
+    last = lax.axis_size("grp") - 1
+    has_low, has_high = region > 0, region < last
+    for there, step in ((has_low, -1), (has_high, 1)):
+        @pl.when(there)
+        def _():
+            pl.semaphore_signal(
+                barrier, inc=1, device_id={"grp": region + step}, device_id_type=MESH
+            )
     own = pltpu.make_async_copy(req_ref.at[me], want_ref.at[me], own_sem)
     own.start()
     lane = iota((blocks, LANES), 1)
@@ -87,9 +101,11 @@
 
     for c in range(5):
         if c == 3:
-            pl.semaphore_wait(barrier, peers - 1)
+            pl.semaphore_wait(
+                barrier, peers - 1 + has_low.astype(jnp.int32) + has_high.astype(jnp.int32)
+            )
             for d in range(1, peers):
-                copy(d).start()
+                request(d).start()
         for (face, half), value in layers(flow_ref, c).items():
             put(face, half, c, value)
         for (face, half), value in layers(adj_ref, c).items():
@@ -103,40 +119,10 @@
                     ref[face, c, :, where] = prim[c]
     own.wait()
     for d in range(1, peers):
-        copy(d).wait()
-
-
-def plan_kernel(capacity, owner_ref, link_ref, req_ref, place_ref, count_ref):
-    def clear(p, carry):
-        count_ref[p] = 0
-        for s in range(capacity):
-            req_ref[p, 0, s] = 0
-        return carry
-
-    lax.fori_loop(0, req_ref.shape[0], clear, 0)
-
-    def ask(b, carry):
-        for f in range(4):
-            owner = owner_ref[f, 0, b]
-            at = count_ref[owner]
-            count_ref[owner] = at + 1
-            req_ref[owner, 0, at] = link_ref[f, b] // 5 * 4 + (f ^ 1)
-            place_ref[b * 4 + f] = owner * 4096 + at
-        return carry
-
-    lax.fori_loop(0, link_ref.shape[1], ask, 0)
-
-
-def exchange_kernel(
-    capacity, want_ref, lat_ref, ver_ref, ret_ref, low_ref, high_ref,
-    stage, send_sem, recv_sem, up_sem, down_sem,
-):
-    peers = ret_ref.shape[0]
-    me = lax.axis_index("blk")
-    region = lax.axis_index("grp")
-    last = lax.axis_size("grp") - 1
-    has_low, has_high = region > 0, region < last
-
+        request(d).wait()
+    indices = pltpu.make_async_copy(want_ref, index_ref, own_sem)
+    indices.start()
+    indices.wait()
     def copy(d):
         peer = lax.rem(me + d, peers)
         return pltpu.make_async_remote_copy(
@@ -160,21 +146,9 @@
 
     upward = vertical(1, low_ref, up_sem, 1)
     downward = vertical(0, high_ref, down_sem, -1)
-    barrier = pltpu.get_barrier_semaphore()
-    for d in range(1, peers):
-        pl.semaphore_signal(
-            barrier, inc=1, device_id={"blk": lax.rem(me + d, peers)}, device_id_type=MESH
-        )
-    for there, step in ((has_low, -1), (has_high, 1)):
-        @pl.when(there)
-        def _():
-            pl.semaphore_signal(
-                barrier, inc=1, device_id={"grp": region + step}, device_id_type=MESH
-            )
-
     def gather(peer, ref, at):
         def one(s, carry):
-            code = want_ref[peer, 0, s]
+            code = index_ref[peer, 0, s]
             face, block = code & 3, code >> 2
             for c in range(10):
                 ref[at, pl.ds(s * 10 + c, 1), :] = lat_ref[face, c, pl.ds(block, 1), :]
@@ -187,9 +161,14 @@
         gather(peer, stage, peer)
 
     fill(1)
-    pl.semaphore_wait(
-        barrier, peers - 1 + has_low.astype(jnp.int32) + has_high.astype(jnp.int32)
-    )
+
+    @pl.when(has_high)
+    def _():
+        upward.start()
+
+    @pl.when(has_low)
+    def _():
+        downward.start()
 
     def send(d, carry):
         fill(d)
@@ -197,20 +176,15 @@
         return carry
 
     lax.fori_loop(2, peers, send, 0)
-    gather(me, ret_ref, me)
+    gather(me, stage, me)
     copy(peers - 1).start()
-
-    @pl.when(has_high)
-    def _():
-        upward.start()
-
-    @pl.when(has_low)
-    def _():
-        downward.start()
 
     def far(ref):
         for c in range(10):
             ref[c] = jnp.full(ref.shape[1:], FREESTREAM[c] if c < 5 else 0.0, jnp.float32)
+
+    mine = pltpu.make_async_copy(stage.at[me], ret_ref.at[me], own_sem)
+    mine.start()
 
     @pl.when(has_low)
     def _():
@@ -235,6 +209,28 @@
         return carry
 
     lax.fori_loop(1, peers, finish, 0)
+    mine.wait()
+
+
+def plan_kernel(capacity, owner_ref, link_ref, req_ref, place_ref, count_ref):
+    def clear(p, carry):
+        count_ref[p] = 0
+        for s in range(capacity):
+            req_ref[p, 0, s] = 0
+        return carry
+
+    lax.fori_loop(0, req_ref.shape[0], clear, 0)
+
+    def ask(b, carry):
+        for f in range(4):
+            owner = owner_ref[f, 0, b]
+            at = count_ref[owner]
+            count_ref[owner] = at + 1
+            req_ref[owner, 0, at] = link_ref[f, b] // 5 * 4 + (f ^ 1)
+            place_ref[b * 4 + f] = owner * 4096 + at
+        return carry
+
+    lax.fori_loop(0, link_ref.shape[1], ask, 0)
 
 
 def minmod(a, b):
@@ -328,8 +324,9 @@
 
 def main_kernel(
     place_ref, link_ref, ver_link_ref,
-    flow_ref, adj_ref, flag_ref, ret_ref, low_ref, high_ref,
+    flow_ref, adj_ref, flag_ref, ret_hbm, low_hbm, high_hbm,
     out_ref,
+    ret_ref, low_ref, high_ref, sems,
     val, slope, solid, ghost, low_k, low_j, mom_k, mom_j, mom_i, lo_solid,
 ):
     blocks = flow_ref.shape[1]
@@ -373,7 +370,13 @@
             solid[g, 1 + i] = x.astype(jnp.float32)
         return carry
 
+    pairs = ((ret_hbm, ret_ref), (low_hbm, low_ref), (high_hbm, high_ref))
+    copies = [pltpu.make_async_copy(a, b, sems.at[at]) for at, (a, b) in enumerate(pairs)]
+    for copy in copies:
+        copy.start()
     lax.fori_loop(0, EDGE, load_layer, 0)
+    for copy in copies:
+        copy.wait()
 
     def load_ghost(c, carry):
         for b in range(blocks):
@@ -585,51 +588,38 @@
         name="plan",
     )(owner_t, link_t)
 
-    lateral, vertical, wanted = pl.pallas_call(
-        faces_kernel,
-        out_shape=(
-            f32((4, 10, blocks, PLANE)),
-            f32((2, 10, blocks, PLANE)),
-            i32((peers, 1, LANES)),
-        ),
+    received = (peers, capacity * 10, PLANE)
+    returned, from_low, from_high = pl.pallas_call(
+        functools.partial(halo_kernel, capacity),
+        out_shape=(f32(received), f32((10, blocks, PLANE)), f32((10, blocks, PLANE))),
         in_specs=[VMEM] * 3,
-        out_specs=(VMEM,) * 3,
+        out_specs=(HBM, VMEM, VMEM),
         scratch_shapes=[
-            pltpu.SemaphoreType.DMA((peers,)),
-            pltpu.SemaphoreType.DMA((peers,)),
+            pltpu.VMEM((4, 10, blocks, PLANE), jnp.float32),
+            pltpu.VMEM((2, 10, blocks, PLANE), jnp.float32),
+            pltpu.VMEM((peers, 1, LANES), jnp.int32),
+            pltpu.SMEM((peers, 1, LANES), jnp.int32),
+            pltpu.VMEM(received, jnp.float32),
+            *[pltpu.SemaphoreType.DMA((peers,))] * 4,
+            pltpu.SemaphoreType.DMA((2,)),
+            pltpu.SemaphoreType.DMA((2,)),
             pltpu.SemaphoreType.DMA,
         ],
         compiler_params=pltpu.CompilerParams(collective_id=0, has_side_effects=True),
-        name="faces",
+        name="halo",
     )(requests, flow_t, adj_t)
-
-    returned, from_low, from_high = pl.pallas_call(
-        functools.partial(exchange_kernel, capacity),
-        out_shape=(
-            f32((peers, capacity * 10, PLANE)),
-            f32((10, blocks, PLANE)),
-            f32((10, blocks, PLANE)),
-        ),
-        in_specs=[SMEM, VMEM, VMEM],
-        out_specs=(VMEM,) * 3,
-        scratch_shapes=[
-            pltpu.VMEM((peers, capacity * 10, PLANE), jnp.float32),
-            pltpu.SemaphoreType.DMA((peers,)),
-            pltpu.SemaphoreType.DMA((peers,)),
-            pltpu.SemaphoreType.DMA((2,)),
-            pltpu.SemaphoreType.DMA((2,)),
-        ],
-        compiler_params=pltpu.CompilerParams(collective_id=1, has_side_effects=True),
-        name="exchange",
-    )(wanted, lateral, vertical)
 
     tile = functools.partial(pltpu.VMEM, dtype=jnp.float32)
     return pl.pallas_call(
         main_kernel,
         out_shape=f32((blocks, EDGE * PLANE)),
-        in_specs=[SMEM] * 3 + [VMEM] * 6,
+        in_specs=[SMEM] * 3 + [VMEM] * 3 + [HBM] * 3,
         out_specs=VMEM,
         scratch_shapes=[
+            tile(received),
+            tile((10, blocks, PLANE)),
+            tile((10, blocks, PLANE)),
+            pltpu.SemaphoreType.DMA((3,)),
             tile((groups, 10, EDGE + 2, 8, LANES)),
             tile((3, 10, EDGE + 2, 8, LANES)),
             tile((groups, EDGE + 2, 8, LANES)),

time: 84.6 us -> 81.5 us (0.963); the launches traced: 83.4 us -> 81.3 us
  Pallas kernels: 80.3 us -> 77.2 us
  local copies, waits for them, and re-layouts: 2.99 us -> 3.94 us
    pallas_call x2 -> x1, Pallas kernels: 33 us -> 29.4 us  [local(): pl.pallas_call(functools.partial(halo_kernel, capacity), out_shape=(f32(r...]
    unnamed x18, local copies, waits for them, and re-layouts: 2.99 us -> 3.94 us
where the time goes in v3:
time: 81.5 us; the launch traced here: 81.3 us
  Pallas kernels  77.2 us (95%)
  local copies, waits for them, and re-layouts  3.94 us (5%)
    pallas_call x1, Pallas kernels, local(): pl.pallas_call(main_kernel, out_shape=f32((blocks, EDGE * PLANE)), in_spe...  45.8 us
    pallas_call x1, Pallas kernels, local(): pl.pallas_call(functools.partial(halo_kernel, capacity), out_shape=(f32(r...  29.4 us
    unnamed x18, local copies, waits for them, and re-layouts  3.94 us
    pallas_call x1, Pallas kernels, local(): pl.pallas_call(functools.partial(plan_kernel, capacity), out_shape=(i32((...  1.96 us

profile of v3, /device:TPU:14, one launch (start us, length us, event | category | flops | bytes accessed | tf_op | source)
XLA Modules:
  0.0 81.3 jit_solution(1270687479914149981)
XLA Ops:
  0.0 2.0 %plan.1 = (s32[8,1,128]{2,1,0:T(1,128)}, s32[48]{0:T(128)}) custom-call(s32[4,1,12]{2,1,0:T(1,128)} %bitcast.12, s32[4,12]{1,0:T(4,128)} %bitcast.9), custom_call_target="tpu_custom_call" | custom-call | tf_op jit(solution)/shard_map/plan/pallas_call | solution.py:582
  2.0 0.0 copy-start
  2.0 0.0 copy-start.1
  2.0 0.0 copy-start.6
  2.0 0.0 copy-start.7
  2.0 0.0 copy-start.8
  2.0 29.4 %halo.1 = (f32[8,90,256]{2,1,0:T(8,128)}, f32[10,12,256]{2,1,0:T(8,128)}, f32[10,12,256]{2,1,0:T(8,128)}) custom-call(s32[8,1,128]{2,1,0:T(1,128)} %get-tuple-element.11.req_ref, f32[5,12,4096]{2,1,0:T(8,128)} %bitcast.5, f32[5,12,4096]{2,1,0:T(8,128)} %bitcast.7), custom_call_target="tpu_custom_call" | custom-call | tf_op jit(solution)/shard_map/halo/pallas_call | solution.py:592
  31.5 0.0 copy-done
  31.5 0.0 copy-done.1
  31.5 0.0 copy-done.6
  31.5 0.0 copy-done.7
  31.5 0.0 copy-done.8
  31.5 0.0 copy-start.2
  31.5 1.1 %copy-done.2 = f32[8,90,256]{2,1,0:T(8,128)S(1)} copy-done((f32[8,90,256]{2,1,0:T(8,128)S(1)}, f32[8,90,256]{2,1,0:T(8,128)}, u32[]{:S(2)}) %copy-start.2) | copy-done | bytes 737304
  32.7 0.0 copy-start.3
  32.7 0.9 %copy-done.3 = s32[12,4096]{1,0:T(8,128)S(1)} copy-done((s32[12,4096]{1,0:T(8,128)S(1)}, s32[12,4096]{1,0:T(8,128)}, u32[]{:S(2)}) %copy-start.3) | copy-done | bytes 196632
  33.6 0.0 copy-start.4
  33.6 0.9 %copy-done.4 = f32[10,12,256]{2,1,0:T(8,128)S(1)} copy-done((f32[10,12,256]{2,1,0:T(8,128)S(1)}, f32[10,12,256]{2,1,0:T(8,128)}, u32[]{:S(2)}) %copy-start.4) | copy-done | bytes 122904
  34.5 0.0 copy-start.5
  34.5 0.9 %copy-done.5 = f32[10,12,256]{2,1,0:T(8,128)S(1)} copy-done((f32[10,12,256]{2,1,0:T(8,128)S(1)}, f32[10,12,256]{2,1,0:T(8,128)}, u32[]{:S(2)}) %copy-start.5) | copy-done | bytes 122904
  35.4 45.8 %indicator.1 = f32[12,4096]{1,0:T(8,128)} custom-call(s32[48]{0:T(128)S(1)} %copy-done.8, s32[4,12]{1,0:T(4,128)S(1)} %bitcast.10, s32[2,12]{1,0:T(2,128)S(1)} %bitcast.11, f32[5,12,4096]{2,1,0:T(8,128)S(1)} %bitcast.6, f32[5,12,4096]{2,1,0:T(8,128)S(1)} %bitcast.8, s32[12,4096]{1,0:T(8,128)S(1)} %copy-done.3, f32[8,90,256]{2,1,0:T(8,128)S(1)} %copy-done.2, ...), custom_call_target="tpu_custom_call" | custom-call | tf_op jit(solution)/shard_map/indicator/pallas_call | solution.py:613
Async XLA Ops:
  2.0 29.5 %copy-start = (f32[12,5,4096]{2,0,1:T(8,128)S(1)}, f32[12,5,4096]{2,0,1:T(8,128)}, u32[]{:S(2)}) copy-start(f32[12,5,4096]{2,0,1:T(8,128)} %param.6) | copy-start | bytes 2949124
  2.0 29.5 %copy-start.1 = (f32[12,5,4096]{2,0,1:T(8,128)S(1)}, f32[12,5,4096]{2,0,1:T(8,128)}, u32[]{:S(2)}) copy-start(f32[12,5,4096]{2,0,1:T(8,128)} %param.7) | copy-start | bytes 2949124
  2.0 29.5 %copy-start.6 = (s32[12,4]{0,1:T(4,128)S(1)}, s32[12,4]{0,1:T(4,128)}, u32[]{:S(2)}) copy-start(s32[12,4]{0,1:T(4,128)} %param.10) | copy-start | bytes 580
  2.0 29.5 %copy-start.7 = (s32[12,2]{0,1:T(2,128)S(1)}, s32[12,2]{0,1:T(2,128)}, u32[]{:S(2)}) copy-start(s32[12,2]{0,1:T(2,128)} %param.11) | copy-start | bytes 292
  2.0 29.5 %copy-start.8 = (s32[48]{0:T(128)S(1)}, s32[48]{0:T(128)}, u32[]{:S(2)}) copy-start(s32[48]{0:T(128)} %get-tuple-element.10.place_ref) | copy-start | bytes 580
  31.5 1.1 %copy-start.2 = (f32[8,90,256]{2,1,0:T(8,128)S(1)}, f32[8,90,256]{2,1,0:T(8,128)}, u32[]{:S(2)}) copy-start(f32[8,90,256]{2,1,0:T(8,128)} %get-tuple-element.12.ret_hbm) | copy-start | bytes 2211844
  32.7 0.9 %copy-start.3 = (s32[12,4096]{1,0:T(8,128)S(1)}, s32[12,4096]{1,0:T(8,128)}, u32[]{:S(2)}) copy-start(s32[12,4096]{1,0:T(8,128)} %flag_ref.1) | copy-start | bytes 589828
  33.6 0.9 %copy-start.4 = (f32[10,12,256]{2,1,0:T(8,128)S(1)}, f32[10,12,256]{2,1,0:T(8,128)}, u32[]{:S(2)}) copy-start(f32[10,12,256]{2,1,0:T(8,128)} %get-tuple-element.13.low_hbm) | copy-start | bytes 368644
  34.5 0.9 %copy-start.5 = (f32[10,12,256]{2,1,0:T(8,128)S(1)}, f32[10,12,256]{2,1,0:T(8,128)}, u32[]{:S(2)}) copy-start(f32[10,12,256]{2,1,0:T(8,128)} %get-tuple-element.14.high_hbm) | copy-start | bytes 368644

commit v4 on v3

--- a/solution.py
+++ b/solution.py
@@ -31,10 +31,52 @@
     return [density, *vel, 0.4 * (energy - 0.5 * density * square)]
 
 
+def pack_cells(flow_ref, adj_ref, flag_ref, val_ref, solid_ref):
+    blocks = flow_ref.shape[1]
+    groups = blocks // PACK
+    top = iota((8, LANES), 0) < PACK
+
+    def pack(parts):
+        tiles = []
+        for g in range(groups):
+            at = g * PACK % 8
+            first, second = parts[g * PACK // 8]
+            if first.shape[0] == PACK:
+                tiles.append(jnp.concatenate([first, second], axis=0))
+            elif at == 0:
+                tiles.append(jnp.where(top, first, pltpu.roll(second, 4, 0)))
+            else:
+                tiles.append(jnp.where(top, pltpu.roll(first, 4, 0), second))
+        return tiles
+
+    def read(load, i):
+        parts = []
+        for start in range(0, blocks, 8):
+            rows = slice(start, min(start + 8, blocks))
+            parts.append(
+                [load(rows, pl.ds(pl.multiple_of(i * PLANE + h * LANES, LANES), LANES)) for h in range(2)]
+            )
+        return pack(parts)
+
+    def load_layer(i, carry):
+        flow = [read(lambda r, s: flow_ref[c, r, s], i) for c in range(5)]
+        for g in range(groups):
+            for c, x in enumerate(primitive([f[g] for f in flow])):
+                val_ref[g, c, i] = x
+        for c in range(5):
+            for g, x in enumerate(read(lambda r, s: adj_ref[c, r, s], i)):
+                val_ref[g, 5 + c, i] = x
+        for g, x in enumerate(read(lambda r, s: flag_ref[r, s], i)):
+            solid_ref[g, i] = x.astype(jnp.float32)
+        return carry
+
+    lax.fori_loop(0, EDGE, load_layer, 0)
+
+
 def halo_kernel(
-    capacity, req_ref, flow_ref, adj_ref, ret_ref, low_ref, high_ref,
+    capacity, req_ref, flow_ref, adj_ref, flag_ref, ret_ref, low_ref, high_ref, val_hbm, solid_hbm,
     lat_ref, ver_ref, want_ref, index_ref, stage,
-    ask_sem, asked_sem, send_sem, recv_sem, up_sem, down_sem, own_sem,
+    ask_sem, asked_sem, send_sem, recv_sem, up_sem, down_sem, own_sem, val_ref, solid_ref, pack_sem,
 ):
     blocks = flow_ref.shape[1]
     peers = req_ref.shape[0]
@@ -185,6 +227,7 @@
 
     mine = pltpu.make_async_copy(stage.at[me], ret_ref.at[me], own_sem)
     mine.start()
+    pack_cells(flow_ref, adj_ref, flag_ref, val_ref, solid_ref)
 
     @pl.when(has_low)
     def _():
@@ -204,12 +247,21 @@
     def _():
         far(high_ref)
 
+    packed = [
+        pltpu.make_async_copy(val_ref, val_hbm, pack_sem.at[0]),
+        pltpu.make_async_copy(solid_ref, solid_hbm, pack_sem.at[1]),
+    ]
+    for copy_out in packed:
+        copy_out.start()
+
     def finish(d, carry):
         copy(d).wait()
         return carry
 
     lax.fori_loop(1, peers, finish, 0)
     mine.wait()
+    for copy_out in packed:
+        copy_out.wait()
 
 
 def plan_kernel(capacity, owner_ref, link_ref, req_ref, place_ref, count_ref):
@@ -324,57 +376,27 @@
 
 def main_kernel(
     place_ref, link_ref, ver_link_ref,
-    flow_ref, adj_ref, flag_ref, ret_hbm, low_hbm, high_hbm,
+    ret_hbm, low_hbm, high_hbm, val_hbm, solid_hbm,
     out_ref,
     ret_ref, low_ref, high_ref, sems,
     val, slope, solid, ghost, low_k, low_j, mom_k, mom_j, mom_i, lo_solid,
 ):
-    blocks = flow_ref.shape[1]
+    blocks = link_ref.shape[1]
     groups = blocks // PACK
     lane = iota((8, LANES), 1)
     row = iota((8, LANES), 0)
     top = row < PACK
     slot, spot = lane >> 4, lane & 15
 
-    def pack(parts):
-        tiles = []
-        for g in range(groups):
-            at = g * PACK % 8
-            first, second = parts[g * PACK // 8]
-            if first.shape[0] == PACK:
-                tiles.append(jnp.concatenate([first, second], axis=0))
-            elif at == 0:
-                tiles.append(jnp.where(top, first, pltpu.roll(second, 4, 0)))
-            else:
-                tiles.append(jnp.where(top, pltpu.roll(first, 4, 0), second))
-        return tiles
-
-    def read(load, i):
-        parts = []
-        for start in range(0, blocks, 8):
-            rows = slice(start, min(start + 8, blocks))
-            parts.append(
-                [load(rows, pl.ds(pl.multiple_of(i * PLANE + h * LANES, LANES), LANES)) for h in range(2)]
-            )
-        return pack(parts)
-
-    def load_layer(i, carry):
-        flow = [read(lambda r, s: flow_ref[c, r, s], i) for c in range(5)]
-        for g in range(groups):
-            for c, x in enumerate(primitive([f[g] for f in flow])):
-                val[g, c, 1 + i] = x
-        for c in range(5):
-            for g, x in enumerate(read(lambda r, s: adj_ref[c, r, s], i)):
-                val[g, 5 + c, 1 + i] = x
-        for g, x in enumerate(read(lambda r, s: flag_ref[r, s], i)):
-            solid[g, 1 + i] = x.astype(jnp.float32)
-        return carry
-
     pairs = ((ret_hbm, ret_ref), (low_hbm, low_ref), (high_hbm, high_ref))
     copies = [pltpu.make_async_copy(a, b, sems.at[at]) for at, (a, b) in enumerate(pairs)]
-    for copy in copies:
+    inside = pl.ds(1, EDGE)
+    cells = [
+        pltpu.make_async_copy(val_hbm, val.at[:, :, inside], sems.at[3]),
+        pltpu.make_async_copy(solid_hbm, solid.at[:, inside], sems.at[4]),
+    ]
+    for copy in copies + cells:
         copy.start()
-    lax.fori_loop(0, EDGE, load_layer, 0)
     for copy in copies:
         copy.wait()
 
@@ -424,6 +446,9 @@
             nothing = jnp.zeros((8, LANES), jnp.float32)
             slope[d, c, 0] = nothing
             slope[d, c, EDGE + 1] = nothing
+
+    for copy in cells:
+        copy.wait()
 
     def next_k(x, edge, i):
         edge = 0.0 if edge is None else pltpu.roll(edge, 15 - i, 1)
@@ -589,11 +614,19 @@
     )(owner_t, link_t)
 
     received = (peers, capacity * 10, PLANE)
-    returned, from_low, from_high = pl.pallas_call(
+    cells = (groups, 10, EDGE, 8, LANES)
+    flags = (groups, EDGE, 8, LANES)
+    returned, from_low, from_high, packed, solid = pl.pallas_call(
         functools.partial(halo_kernel, capacity),
-        out_shape=(f32(received), f32((10, blocks, PLANE)), f32((10, blocks, PLANE))),
-        in_specs=[VMEM] * 3,
-        out_specs=(HBM, VMEM, VMEM),
+        out_shape=(
+            f32(received),
+            f32((10, blocks, PLANE)),
+            f32((10, blocks, PLANE)),
+            f32(cells),
+            f32(flags),
+        ),
+        in_specs=[VMEM] * 4,
+        out_specs=(HBM, VMEM, VMEM, HBM, HBM),
         scratch_shapes=[
             pltpu.VMEM((4, 10, blocks, PLANE), jnp.float32),
             pltpu.VMEM((2, 10, blocks, PLANE), jnp.float32),
@@ -604,22 +637,25 @@
             pltpu.SemaphoreType.DMA((2,)),
             pltpu.SemaphoreType.DMA((2,)),
             pltpu.SemaphoreType.DMA,
+            pltpu.VMEM(cells, jnp.float32),
+            pltpu.VMEM(flags, jnp.float32),
+            pltpu.SemaphoreType.DMA((2,)),
         ],
         compiler_params=pltpu.CompilerParams(collective_id=0, has_side_effects=True),
         name="halo",
-    )(requests, flow_t, adj_t)
+    )(requests, flow_t, adj_t, cut_flag)
 
     tile = functools.partial(pltpu.VMEM, dtype=jnp.float32)
     return pl.pallas_call(
         main_kernel,
         out_shape=f32((blocks, EDGE * PLANE)),
-        in_specs=[SMEM] * 3 + [VMEM] * 3 + [HBM] * 3,
+        in_specs=[SMEM] * 3 + [HBM] * 5,
         out_specs=VMEM,
         scratch_shapes=[
             tile(received),
             tile((10, blocks, PLANE)),
             tile((10, blocks, PLANE)),
-            pltpu.SemaphoreType.DMA((3,)),
+            pltpu.SemaphoreType.DMA((5,)),
             tile((groups, 10, EDGE + 2, 8, LANES)),
             tile((3, 10, EDGE + 2, 8, LANES)),
             tile((groups, EDGE + 2, 8, LANES)),
@@ -631,11 +667,11 @@
             tile((15, 8, LANES)),
             tile((groups, EDGE, 8, LANES)),
         ],
-        compiler_params=pltpu.CompilerParams(vmem_limit_bytes=50 * 1024 * 1024),
+        compiler_params=pltpu.CompilerParams(vmem_limit_bytes=63 * 1024 * 1024),
         name="indicator",
     )(
         place, link_t, ver_link_t,
-        flow_t, adj_t, cut_flag, returned, from_low, from_high,
+        returned, from_low, from_high, packed, solid,
     )
 
 

time: 81.5 us -> 77.7 us (0.953)
  local copies, waits for them, and re-layouts: 3.94 us -> 0 us
    unnamed x18 -> x0, local copies, waits for them, and re-layouts: 3.94 us -> none
where the time goes in v4:
time: 77.7 us; the launch traced here: 77.5 us
  Pallas kernels  77.5 us (100%)
    pallas_call x1, Pallas kernels, local(): pl.pallas_call(main_kernel, out_shape=f32((blocks, EDGE * PLANE)), in_spe...  46.2 us
    pallas_call x1, Pallas kernels, local(): pl.pallas_call(functools.partial(halo_kernel, capacity), out_shape=(f32(r...  29.3 us
    pallas_call x1, Pallas kernels, local(): pl.pallas_call(functools.partial(plan_kernel, capacity), out_shape=(i32((...  1.96 us

profile of v4, /device:TPU:14, one launch (start us, length us, event | category | flops | bytes accessed | tf_op | source)
XLA Modules:
  0.0 77.5 jit_solution(13633413059279373300)
XLA Ops:
  0.0 2.0 %plan.1 = (s32[8,1,128]{2,1,0:T(1,128)}, s32[48]{0:T(128)}) custom-call(s32[4,1,12]{2,1,0:T(1,128)} %bitcast.9, s32[4,12]{1,0:T(4,128)} %bitcast.7), custom_call_target="tpu_custom_call" | custom-call | tf_op jit(solution)/shard_map/plan/pallas_call | solution.py:607
  2.0 29.3 %halo.1 = (f32[8,90,256]{2,1,0:T(8,128)}, f32[10,12,256]{2,1,0:T(8,128)}, f32[10,12,256]{2,1,0:T(8,128)}, f32[3,10,16,8,128]{4,3,2,1,0:T(8,128)}, f32[3,16,8,128]{3,2,1,0:T(8,128)}) custom-call(s32[8,1,128]{2,1,0:T(1,128)} %get-tuple-element.13.req_ref, f32[5,12,4096]{2,1,0:T(8,128)} %bitcast.5, f32[5,12,4096]{2,1,0:T(8,128)} %bitcast.6, s32[12,4096]{1,0:T(8,128)} %flag_ref.1), custom_call_target="tpu_custom_call" | custom-call | tf_op jit(solution)/shard_map/halo/pallas_call | solution.py:619
  31.3 46.2 %indicator.1 = f32[12,4096]{1,0:T(8,128)} custom-call(s32[48]{0:T(128)} %get-tuple-element.12.place_ref, s32[4,12]{1,0:T(4,128)} %bitcast.8, s32[2,12]{1,0:T(2,128)} %bitcast.10, f32[8,90,256]{2,1,0:T(8,128)} %get-tuple-element.14.ret_hbm, f32[10,12,256]{2,1,0:T(8,128)} %get-tuple-element.15.low_hbm, f32[10,12,256]{2,1,0:T(8,128)} %get-tuple-element.16.high_hbm, ...), custom_call_target="tpu_custom_call" | custom-call | tf_op jit(solution)/shard_map/indicator/pallas_call | solution.py:649
